TPU v7x, 256 devices: a whole 4x4x8 slice. The times are simulated.
256 devices in a mesh: lat: 4 (over y_lo, core), lon: 64 (over z, x, y_hi).
Axes of the slice: x: 4, y: 4 (y_hi: 2, y_lo: 2; y = y_hi * 2 + y_lo), z: 8, core: 2. Of those that a mesh axis runs over, the one named last changes fastest.
Arguments:
- residual: bfloat16 [128, 1024, 128], P('lat', 'lon'), may hold values from -6 to 6
- noise_weights: float32 [128, 1024], P('lat', 'lon'), may hold values from 0.5 to 4
- kernel: bfloat16 [4, 1, 2048, 2048], P(None, None, 'lat'), may hold values from -0.0625 to 0.0625
Outputs:
- gradient: float32 [1, 128, 1024, 128], P(None, 'lat', 'lon')
All inputs are finite; a program needn't handle non-finite values.
Results may differ from a plain program's by a relative error of at most 0.0029.
Values may be sent and summed in bfloat16 or wider, within the bound.
No kernel may reach another device: no remote copies, remote signals or barrier semaphores. Data moves between devices by JAX's collectives and lax.ppermute only.
A program may use at most 64 MiB of HBM per device.

v0:
```python
import jax
import jax.numpy as jnp
from jax import lax
from jax.experimental import pallas as pl
from jax.experimental.pallas import tpu as pltpu
from jax.sharding import PartitionSpec as P


VMEM = pl.BlockSpec(memory_space=pltpu.VMEM)
HBM = pl.BlockSpec(memory_space=pltpu.HBM)


def in_hbm(value):
    return pltpu.with_memory_space_constraint(value, pltpu.HBM)


def eastward(value, by):
    length = lax.axis_size("lon")
    return lax.ppermute(value, "lon", [(i, (i + by) % length) for i in range(length)])


def swapped(value, mask):
    length = lax.axis_size("lat")
    return lax.ppermute(value, "lat", [(i, i ^ mask) for i in range(length)])


def call(body, outs, in_specs, scratch, flops, nbytes, limit):
    return pl.pallas_call(
        body,
        out_shape=outs,
        in_specs=in_specs,
        out_specs=jax.tree.map(lambda _: VMEM, outs),
        scratch_shapes=scratch,
        cost_estimate=pl.CostEstimate(flops=flops, bytes_accessed=nbytes, transcendentals=0),
        compiler_params=pltpu.CompilerParams(vmem_limit_bytes=limit),
    )


def weigh_body(residual, noise, out, data, weights, sems):
    copies = [
        pltpu.make_async_copy(noise, weights, sems.at[0]),
        pltpu.make_async_copy(residual, data, sems.at[1]),
    ]
    for copy in copies:
        copy.start()
    for copy in copies:
        copy.wait()
    part = [
        (weights[:, y : y + 1] * data[y].astype(jnp.float32)).astype(out.dtype)
        for y in range(data.shape[0])
    ]
    out[...] = jnp.concatenate(part, axis=0).T


def first_body(weighted, panels, acc, own, sems):
    cells = weighted.shape[1]
    depth = cells // sems.shape[0]
    copies = [
        pltpu.make_async_copy(
            panels.at[0, 0, pl.ds(i * depth, depth)], own.at[pl.ds(i * depth, depth)], sems.at[i]
        )
        for i in range(sems.shape[0])
    ]
    for copy in copies:
        copy.start()
    for copy in copies:
        copy.wait()
    for k in range(panels.shape[3] // cells):
        where = slice(k * cells, (k + 1) * cells)
        acc[:, where] = jnp.dot(weighted[...], own[:, where], preferred_element_type=jnp.float32)


def band_sum(halo, panels, acc, band, cells):
    where = pl.ds(pl.multiple_of(band * cells, cells), cells)
    total = acc[:, where]
    for d, h in enumerate(halo):
        total += jnp.dot(h[...], panels[d + 1, 0, :, where], preferred_element_type=jnp.float32)
    return total


def far_body(h2, h3, h1, panels, acc, out):
    band = 3 - lax.axis_index("lat")
    out[...] = band_sum((h1, h2, h3), panels, acc, band, h1.shape[1]).astype(out.dtype)


def rest_body(h2, h3, h1, panels, acc, near, mine):
    band = lax.axis_index("lat")
    partner = band + 1 - 2 * (band % 2)
    halo, cells = (h1, h2, h3), h1.shape[1]
    near[...] = band_sum(halo, panels, acc, partner, cells).astype(near.dtype)
    mine[0] = band_sum(halo, panels, acc, 3 - partner, cells)
    mine[1] = band_sum(halo, panels, acc, band, cells)


def pack_body(mine, other, out):
    out[...] = (mine[0] + other[...].astype(jnp.float32)).astype(out.dtype)


def final_body(mine, other, third, out):
    total = mine[1] + other[...].astype(jnp.float32) + third[...].astype(jnp.float32)
    out[...] = total.T


def sweep(residual, noise_weights, kernel):
    rows, columns, probes = residual.shape
    cells = rows * columns
    every = kernel.shape[3]
    f32, bf16 = jnp.float32, jnp.bfloat16
    shape = jax.ShapeDtypeStruct
    MB = 1 << 20

    weighted = call(
        weigh_body,
        pltpu.VMEM((probes, cells), bf16),
        [HBM] * 2,
        [
            pltpu.VMEM((rows, columns, probes), bf16),
            pltpu.VMEM((columns, rows), f32),
            pltpu.SemaphoreType.DMA((2,)),
        ],
        0,
        MB // 4,
        58 * MB,
    )(in_hbm(residual), in_hbm(noise_weights.T))
    h1, h3, h2 = [eastward(weighted, by) for by in (1, 3, 2)]
    flops = 2 * probes * cells * every
    acc = call(
        first_body,
        shape((probes, every), f32),
        [VMEM, HBM],
        [pltpu.VMEM((cells, every), bf16), pltpu.SemaphoreType.DMA((4,))],
        flops,
        3 * MB,
        8 * MB,
    )(weighted, in_hbm(kernel))
    flops = 6 * probes * cells * cells
    far = call(far_body, shape((probes, cells), bf16), [VMEM] * 5, [], flops, 2 * MB, 8 * MB)(
        h2, h3, h1, kernel, acc
    )
    other_far = swapped(far, 1)
    near, mine = call(
        rest_body,
        (shape((probes, cells), bf16), shape((2, probes, cells), f32)),
        [VMEM] * 5,
        [],
        3 * flops,
        6 * MB,
        8 * MB,
    )(h2, h3, h1, kernel, acc)
    packed = call(pack_body, shape((probes, cells), bf16), [VMEM] * 2, [], 0, MB, 4 * MB)(mine, other_far)
    third = swapped(packed, 2)
    other_near = swapped(near, 1)
    total = call(final_body, shape((cells, probes), f32), [VMEM] * 3, [], 0, MB, 4 * MB)(
        mine, other_near, third
    )
    return total.reshape(1, rows, columns, probes)


def solution(mesh):
    return jax.shard_map(
        sweep,
        mesh=mesh,
        in_specs=(P("lat", "lon", None), P("lat", "lon"), P(None, None, "lat", None)),
        out_specs=P(None, "lat", "lon", None),
        check_vma=False,
    )
```

profile of v0, /device:TPU:1, one launch (start us, length us, event | category | flops | bytes accessed | tf_op | source)
XLA Modules:
  0.0 27.1 jit_solution(1036768539207778857)
XLA Ops:
  0.0 1.2 %shard_map.37.weighted = bf16[128,512]{1,0:T(8,128)(2,1)S(1)} custom-call(bf16[32,16,128]{2,1,0:T(8,128)(2,1)} %residual.1, f32[16,32]{1,0:T(8,128)} %bitcast.2), custom_call_target="tpu_custom_call" | custom-call | bytes 262144 | tf_op jit(solution)/shard_map/pallas_call | solution.py:112
  1.2 0.0 copy-start
  1.2 3.8 %collective-permute-start.2 = (bf16[128,512]{1,0:T(8,128)(2,1)S(1)}, bf16[128,512]{1,0:T(8,128)(2,1)S(1)}, u32[]{:S(2)}, u32[]{:S(2)}) collective-permute-start(bf16[128,512]{1,0:T(8,128)(2,1)S(1)} %shard_map.37.weighted), channel_id=1, source_target_pairs={{0,1},{1,2},{2,3},{3,4},{4,5},{5,6},{6,7},{7,8},{8,9},{9,10},{10,1... | collective-permute-start | bytes 393224 | tf_op jit(solution)/shard_map/ppermute | solution.py:19
  5.0 1.9 %collective-permute-start.1 = (bf16[128,512]{1,0:T(8,128)(2,1)S(1)}, bf16[128,512]{1,0:T(8,128)(2,1)S(1)}, u32[]{:S(2)}, u32[]{:S(2)}) collective-permute-start(bf16[128,512]{1,0:T(8,128)(2,1)S(1)} %shard_map.37.weighted), channel_id=1, source_target_pairs={{0,3},{1,4},{2,5},{3,6},{4,7},{5,8},{6,9},{7,10},{8,11},{9,12},{10... | collective-permute-start | bytes 393224 | tf_op jit(solution)/shard_map/ppermute | solution.py:19
  6.9 0.9 %collective-permute-start = (bf16[128,512]{1,0:T(8,128)(2,1)S(1)}, bf16[128,512]{1,0:T(8,128)(2,1)S(1)}, u32[]{:S(2)}, u32[]{:S(2)}) collective-permute-start(bf16[128,512]{1,0:T(8,128)(2,1)S(1)} %shard_map.37.weighted), channel_id=1, source_target_pairs={{0,2},{1,3},{2,4},{3,5},{4,6},{5,7},{6,8},{7,9},{8,10},{9,11},{10,... | collective-permute-start | bytes 393224 | tf_op jit(solution)/shard_map/ppermute | solution.py:19
  7.8 2.0 %shard_map.38.acc = f32[128,2048]{1,0:T(8,128)S(1)} custom-call(bf16[128,512]{1,0:T(8,128)(2,1)S(1)} %shard_map.37.weighted, bf16[4,1,512,2048]{3,2,1,0:T(8,128)(2,1)} %panels.5), custom_call_target="tpu_custom_call" | custom-call | flops 268435456 | bytes 3145728 | tf_op jit(solution)/shard_map/pallas_call | solution.py:127
  9.8 6.5 %collective-permute-done.2.h1 = bf16[128,512]{1,0:T(8,128)(2,1)S(1)} collective-permute-done((bf16[128,512]{1,0:T(8,128)(2,1)S(1)}, bf16[128,512]{1,0:T(8,128)(2,1)S(1)}, u32[]{:S(2)}, u32[]{:S(2)}) %collective-permute-start.2) | collective-permute-done | bytes 131104 | tf_op jit(solution)/shard_map/ppermute | solution.py:19
  16.3 1.2 %collective-permute-done.1.h3 = bf16[128,512]{1,0:T(8,128)(2,1)S(1)} collective-permute-done((bf16[128,512]{1,0:T(8,128)(2,1)S(1)}, bf16[128,512]{1,0:T(8,128)(2,1)S(1)}, u32[]{:S(2)}, u32[]{:S(2)}) %collective-permute-start.1) | collective-permute-done | bytes 131104 | tf_op jit(solution)/shard_map/ppermute | solution.py:19
  17.6 0.9 %collective-permute-done.h2 = bf16[128,512]{1,0:T(8,128)(2,1)S(1)} collective-permute-done((bf16[128,512]{1,0:T(8,128)(2,1)S(1)}, bf16[128,512]{1,0:T(8,128)(2,1)S(1)}, u32[]{:S(2)}, u32[]{:S(2)}) %collective-permute-start) | collective-permute-done | bytes 131104 | tf_op jit(solution)/shard_map/ppermute | solution.py:19
  18.5 0.0 copy-done
  18.5 0.4 %shard_map.40 = bf16[128,512]{1,0:T(8,128)(2,1)S(1)} custom-call(bf16[128,512]{1,0:T(8,128)(2,1)S(1)} %collective-permute-done.h2, bf16[128,512]{1,0:T(8,128)(2,1)S(1)} %collective-permute-done.1.h3, bf16[128,512]{1,0:T(8,128)(2,1)S(1)} %collective-permute-done.2.h1, bf16[4,1,512,2048]{3,2,1,0:T(8,128)(2,1)S(1)} %copy-done, f32[128,2048]{1,0:T(8,128)S(1)} %shard_map.38.acc), custom_call_target="tpu_custom_call" | custom-call | flops 201326592 | bytes 2097152 | tf_op jit(solution)/shard_map/pallas_call | solution.py:137
  18.9 1.6 %collective-permute-start.4 = (bf16[128,512]{1,0:T(8,128)(2,1)S(1)}, bf16[128,512]{1,0:T(8,128)(2,1)S(1)}, u32[]{:S(2)}, u32[]{:S(2)}) collective-permute-start(bf16[128,512]{1,0:T(8,128)(2,1)S(1)} %shard_map.40), channel_id=1, source_target_pairs={{0,64},{64,0},{128,192},{192,128},{1,65},{65,1},{129,193},{193,129... | collective-permute-start | bytes 393224 | tf_op jit(solution)/shard_map/ppermute | solution.py:24
  20.5 0.8 %shard_map.39 = (bf16[128,512]{1,0:T(8,128)(2,1)S(1)}, f32[2,128,512]{2,1,0:T(8,128)S(1)}) custom-call(bf16[128,512]{1,0:T(8,128)(2,1)S(1)} %collective-permute-done.h2, bf16[128,512]{1,0:T(8,128)(2,1)S(1)} %collective-permute-done.1.h3, bf16[128,512]{1,0:T(8,128)(2,1)S(1)} %collective-permute-done.2.h1, bf16[4,1,512,2048]{3,2,1,0:T(8,128)(2,1)S(1)} %copy-done, ...), custom_call_target="tpu_custom_call" | custom-call | flops 603979776 | bytes 6291456 | tf_op jit(solution)/shard_map/pallas_call | solution.py:141
  21.3 0.1 collective-permute-start.3
  21.4 0.1 collective-permute-done.4.other
  21.5 0.5 %collective-permute-start.5 = (bf16[128,512]{1,0:T(8,128)(2,1)S(1)}, bf16[128,512]{1,0:T(8,128)(2,1)S(1)}, u32[]{:S(2)}, u32[]{:S(2)}) collective-permute-start(bf16[128,512]{1,0:T(8,128)(2,1)S(1)} %shard_map.41), channel_id=1, source_target_pairs={{0,128},{64,192},{128,0},{192,64},{1,129},{65,193},{129,1},{193,65... | collective-permute-start | bytes 393224 | tf_op jit(solution)/shard_map/ppermute | solution.py:24
  22.0 0.7 %collective-permute-done.3.other = bf16[128,512]{1,0:T(8,128)(2,1)S(1)} collective-permute-done((bf16[128,512]{1,0:T(8,128)(2,1)S(1)}, bf16[128,512]{1,0:T(8,128)(2,1)S(1)}, u32[]{:S(2)}, u32[]{:S(2)}) %collective-permute-start.3) | collective-permute-done | bytes 131104 | tf_op jit(solution)/shard_map/ppermute | solution.py:24
  22.7 3.5 %collective-permute-done.5.third = bf16[128,512]{1,0:T(8,128)(2,1)S(1)} collective-permute-done((bf16[128,512]{1,0:T(8,128)(2,1)S(1)}, bf16[128,512]{1,0:T(8,128)(2,1)S(1)}, u32[]{:S(2)}, u32[]{:S(2)}) %collective-permute-start.5) | collective-permute-done | bytes 131104 | tf_op jit(solution)/shard_map/ppermute | solution.py:24
  26.3 0.8 %shard_map.42 = f32[512,128]{1,0:T(8,128)} custom-call(f32[2,128,512]{2,1,0:T(8,128)S(1)} %get-tuple-element.7.mine, bf16[128,512]{1,0:T(8,128)(2,1)S(1)} %collective-permute-done.3.other, bf16[128,512]{1,0:T(8,128)(2,1)S(1)} %collective-permute-done.5.third), custom_call_target="tpu_custom_call" | custom-call | bytes 1048576 | tf_op jit(solution)/shard_map/pallas_call | solution.py:153
  (1 shorter events, 0.0 us)
Async XLA Ops:
  1.2 17.3 %copy-start = (bf16[4,1,512,2048]{3,2,1,0:T(8,128)(2,1)S(1)}, bf16[4,1,512,2048]{3,2,1,0:T(8,128)(2,1)}, u32[]{:S(2)}) copy-start(bf16[4,1,512,2048]{3,2,1,0:T(8,128)(2,1)} %panels.5) | copy-start | bytes 25165828
  1.2 15.2 %collective-permute-start.2 = (bf16[128,512]{1,0:T(8,128)(2,1)S(1)}, bf16[128,512]{1,0:T(8,128)(2,1)S(1)}, u32[]{:S(2)}, u32[]{:S(2)}) collective-permute-start(bf16[128,512]{1,0:T(8,128)(2,1)S(1)} %shard_map.37.weighted), channel_id=1, source_target_pairs={{0,1},{1,2},{2,3},{3,4},{4,5},{5,6},{6,7},{7,8},{8,9},{9,10},{10,1... | collective-permute-start | bytes 393224 | tf_op jit(solution)/shard_map/ppermute | solution.py:19
  5.0 12.6 %collective-permute-start.1 = (bf16[128,512]{1,0:T(8,128)(2,1)S(1)}, bf16[128,512]{1,0:T(8,128)(2,1)S(1)}, u32[]{:S(2)}, u32[]{:S(2)}) collective-permute-start(bf16[128,512]{1,0:T(8,128)(2,1)S(1)} %shard_map.37.weighted), channel_id=1, source_target_pairs={{0,3},{1,4},{2,5},{3,6},{4,7},{5,8},{6,9},{7,10},{8,11},{9,12},{10... | collective-permute-start | bytes 393224 | tf_op jit(solution)/shard_map/ppermute | solution.py:19
  6.9 11.6 %collective-permute-start = (bf16[128,512]{1,0:T(8,128)(2,1)S(1)}, bf16[128,512]{1,0:T(8,128)(2,1)S(1)}, u32[]{:S(2)}, u32[]{:S(2)}) collective-permute-start(bf16[128,512]{1,0:T(8,128)(2,1)S(1)} %shard_map.37.weighted), channel_id=1, source_target_pairs={{0,2},{1,3},{2,4},{3,5},{4,6},{5,7},{6,8},{7,9},{8,10},{9,11},{10,... | collective-permute-start | bytes 393224 | tf_op jit(solution)/shard_map/ppermute | solution.py:19
  18.9 2.6 %collective-permute-start.4 = (bf16[128,512]{1,0:T(8,128)(2,1)S(1)}, bf16[128,512]{1,0:T(8,128)(2,1)S(1)}, u32[]{:S(2)}, u32[]{:S(2)}) collective-permute-start(bf16[128,512]{1,0:T(8,128)(2,1)S(1)} %shard_map.40), channel_id=1, source_target_pairs={{0,64},{64,0},{128,192},{192,128},{1,65},{65,1},{129,193},{193,129... | collective-permute-start | bytes 393224 | tf_op jit(solution)/shard_map/ppermute | solution.py:24
  21.3 1.4 %collective-permute-start.3 = (bf16[128,512]{1,0:T(8,128)(2,1)S(1)}, bf16[128,512]{1,0:T(8,128)(2,1)S(1)}, u32[]{:S(2)}, u32[]{:S(2)}) collective-permute-start(bf16[128,512]{1,0:T(8,128)(2,1)S(1)} %get-tuple-element.8), channel_id=1, source_target_pairs={{0,64},{64,0},{128,192},{192,128},{1,65},{65,1},{129,193},{193,129... | collective-permute-start | bytes 393224 | tf_op jit(solution)/shard_map/ppermute | solution.py:24
  21.5 4.7 %collective-permute-start.5 = (bf16[128,512]{1,0:T(8,128)(2,1)S(1)}, bf16[128,512]{1,0:T(8,128)(2,1)S(1)}, u32[]{:S(2)}, u32[]{:S(2)}) collective-permute-start(bf16[128,512]{1,0:T(8,128)(2,1)S(1)} %shard_map.41), channel_id=1, source_target_pairs={{0,128},{64,192},{128,0},{192,64},{1,129},{65,193},{129,1},{193,65... | collective-permute-start | bytes 393224 | tf_op jit(solution)/shard_map/ppermute | solution.py:24
where the time goes:
time: 27.2 us; the launch traced here: 27.1 us
  waiting for transfers between devices  13 us (48%)
  starting transfers between devices  8.85 us (33%)
  Pallas kernels  5.21 us (19%)
    ppermute x3, waiting for transfers between devices, eastward(): lax.ppermute(value, 'lon', [(i, (i + by) % length) for i in range(length)])  8.66 us
    ppermute x3, starting transfers between devices, eastward(): lax.ppermute(value, 'lon', [(i, (i + by) % length) for i in range(length)])  6.64 us
    ppermute x3, waiting for transfers between devices, swapped(): return lax.ppermute(value, 'lat', [(i, i ^ mask) for i in range(length)])  4.32 us
    ppermute x3, starting transfers between devices, swapped(): return lax.ppermute(value, 'lat', [(i, i ^ mask) for i in range(length)])  2.21 us
    pallas_call x1, Pallas kernels, sweep(): call(first_body, shape((probes, every), f32), [VMEM, HBM], [pltpu.VMEM((c...  2 us
    pallas_call x1, Pallas kernels, sweep(): call(weigh_body, pltpu.VMEM((probes, cells), bf16), [HBM] * 2, [pltpu.VME...  1.16 us
    pallas_call x1, Pallas kernels, sweep(): call(final_body, shape((cells, probes), f32), [VMEM] * 3, [], 0, MB, 4 * MB)  0.84 us
    pallas_call x1, Pallas kernels, sweep(): call(rest_body, (shape((probes, cells), bf16), shape((2, probes, cells),...  0.79 us
  transfers between devices with their start and end apart: 6, of which 6 were waited for; matrix products, arithmetic and copies ran while one was open for 0% of the time, Pallas kernels for 10%

commit v1 on v0

--- a/solution.py
+++ b/solution.py
@@ -14,9 +14,10 @@
     return pltpu.with_memory_space_constraint(value, pltpu.HBM)
 
 
-def eastward(value, by):
+def eastward(value, even, odd):
     length = lax.axis_size("lon")
-    return lax.ppermute(value, "lon", [(i, (i + by) % length) for i in range(length)])
+    pairs = [(i, (i + (odd if i % 2 else even)) % length) for i in range(length)]
+    return lax.ppermute(value, "lon", pairs)
 
 
 def swapped(value, mask):
@@ -72,21 +73,22 @@
 
 def band_sum(halo, panels, acc, band, cells):
     where = pl.ds(pl.multiple_of(band * cells, cells), cells)
+    odd = lax.axis_index("lon") % 2
     total = acc[:, where]
-    for d, h in enumerate(halo):
-        total += jnp.dot(h[...], panels[d + 1, 0, :, where], preferred_element_type=jnp.float32)
+    for d, h in zip((3 - 2 * odd, 1 + 2 * odd, 2), halo):
+        total += jnp.dot(h[...], panels[d, 0, :, where], preferred_element_type=jnp.float32)
     return total
 
 
-def far_body(h2, h3, h1, panels, acc, out):
+def far_body(h2, hb, ha, panels, acc, out):
     band = 3 - lax.axis_index("lat")
-    out[...] = band_sum((h1, h2, h3), panels, acc, band, h1.shape[1]).astype(out.dtype)
+    out[...] = band_sum((ha, hb, h2), panels, acc, band, h2.shape[1]).astype(out.dtype)
 
 
-def rest_body(h2, h3, h1, panels, acc, near, mine):
+def rest_body(h2, hb, ha, panels, acc, near, mine):
     band = lax.axis_index("lat")
     partner = band + 1 - 2 * (band % 2)
-    halo, cells = (h1, h2, h3), h1.shape[1]
+    halo, cells = (ha, hb, h2), h2.shape[1]
     near[...] = band_sum(halo, panels, acc, partner, cells).astype(near.dtype)
     mine[0] = band_sum(halo, panels, acc, 3 - partner, cells)
     mine[1] = band_sum(halo, panels, acc, band, cells)
@@ -122,7 +124,9 @@
         MB // 4,
         58 * MB,
     )(in_hbm(residual), in_hbm(noise_weights.T))
-    h1, h3, h2 = [eastward(weighted, by) for by in (1, 3, 2)]
+    ha = eastward(weighted, 1, 3)
+    hb = eastward(weighted, 3, 1)
+    h2 = eastward(weighted, 2, 2)
     flops = 2 * probes * cells * every
     acc = call(
         first_body,
@@ -135,7 +139,7 @@
     )(weighted, in_hbm(kernel))
     flops = 6 * probes * cells * cells
     far = call(far_body, shape((probes, cells), bf16), [VMEM] * 5, [], flops, 2 * MB, 8 * MB)(
-        h2, h3, h1, kernel, acc
+        h2, hb, ha, kernel, acc
     )
     other_far = swapped(far, 1)
     near, mine = call(
@@ -146,7 +150,7 @@
         3 * flops,
         6 * MB,
         8 * MB,
-    )(h2, h3, h1, kernel, acc)
+    )(h2, hb, ha, kernel, acc)
     packed = call(pack_body, shape((probes, cells), bf16), [VMEM] * 2, [], 0, MB, 4 * MB)(mine, other_far)
     third = swapped(packed, 2)
     other_near = swapped(near, 1)

time: 27.2 us -> 28.1 us (1.033)
  starting transfers between devices: 8.85 us -> 10.4 us
  waiting for transfers between devices: 13 us -> 12.4 us
    ppermute x3, starting transfers between devices: 2.21 us -> 3.08 us  [swapped(): return lax.ppermute(value, 'lat', [(i, i ^ mask) for i in range(length)])]
    ppermute x3, starting transfers between devices: 6.64 us -> 7.3 us  [eastward(): return lax.ppermute(value, 'lon', pairs)]
    ppermute x3, waiting for transfers between devices: 8.66 us -> 8.07 us  [eastward(): return lax.ppermute(value, 'lon', pairs)]
  transfers between devices with their start and end apart: 6 -> 6, of which waited for: 6 -> 5; matrix products, arithmetic and copies ran while one was open for 0% -> 0% of each run, Pallas kernels for 10% -> 10%
where the time goes in v1:
time: 28.1 us; the launch traced here: 28 us
  waiting for transfers between devices  12.4 us (44%)
  starting transfers between devices  10.4 us (37%)
  Pallas kernels  5.2 us (19%)
    ppermute x3, waiting for transfers between devices, eastward(): return lax.ppermute(value, 'lon', pairs)  8.07 us
    ppermute x3, starting transfers between devices, eastward(): return lax.ppermute(value, 'lon', pairs)  7.3 us
    ppermute x3, waiting for transfers between devices, swapped(): return lax.ppermute(value, 'lat', [(i, i ^ mask) for i in range(length)])  4.32 us
    ppermute x3, starting transfers between devices, swapped(): return lax.ppermute(value, 'lat', [(i, i ^ mask) for i in range(length)])  3.08 us
    pallas_call x1, Pallas kernels, sweep(): call(first_body, shape((probes, every), f32), [VMEM, HBM], [pltpu.VMEM((c...  2 us
    pallas_call x1, Pallas kernels, sweep(): call(weigh_body, pltpu.VMEM((probes, cells), bf16), [HBM] * 2, [pltpu.VME...  1.16 us
    pallas_call x1, Pallas kernels, sweep(): call(final_body, shape((cells, probes), f32), [VMEM] * 3, [], 0, MB, 4 * MB)  0.84 us
    pallas_call x1, Pallas kernels, sweep(): call(rest_body, (shape((probes, cells), bf16), shape((2, probes, cells),...  0.79 us
  transfers between devices with their start and end apart: 6, of which 5 were waited for; matrix products, arithmetic and copies ran while one was open for 0% of the time, Pallas kernels for 10%

profile of v1, /device:TPU:1, one launch (start us, length us, event | category | flops | bytes accessed | tf_op | source)
XLA Modules:
  0.0 28.0 jit_solution(9111438741131090032)
XLA Ops:
  0.0 1.2 %shard_map.37.weighted = bf16[128,512]{1,0:T(8,128)(2,1)S(1)} custom-call(bf16[32,16,128]{2,1,0:T(8,128)(2,1)} %residual.1, f32[16,32]{1,0:T(8,128)} %bitcast.2), custom_call_target="tpu_custom_call" | custom-call | bytes 262144 | tf_op jit(solution)/shard_map/pallas_call | solution.py:114
  1.2 0.0 copy-start
  1.2 3.8 %collective-permute-start.2 = (bf16[128,512]{1,0:T(8,128)(2,1)S(1)}, bf16[128,512]{1,0:T(8,128)(2,1)S(1)}, u32[]{:S(2)}, u32[]{:S(2)}) collective-permute-start(bf16[128,512]{1,0:T(8,128)(2,1)S(1)} %shard_map.37.weighted), channel_id=1, source_target_pairs={{0,1},{1,4},{2,3},{3,6},{4,5},{5,8},{6,7},{7,10},{8,9},{9,12},{10,... | collective-permute-start | bytes 393224 | tf_op jit(solution)/shard_map/ppermute | solution.py:20
  5.0 2.5 %collective-permute-start.1 = (bf16[128,512]{1,0:T(8,128)(2,1)S(1)}, bf16[128,512]{1,0:T(8,128)(2,1)S(1)}, u32[]{:S(2)}, u32[]{:S(2)}) collective-permute-start(bf16[128,512]{1,0:T(8,128)(2,1)S(1)} %shard_map.37.weighted), channel_id=1, source_target_pairs={{0,3},{1,2},{2,5},{3,4},{4,7},{5,6},{6,9},{7,8},{8,11},{9,10},{10,... | collective-permute-start | bytes 393224 | tf_op jit(solution)/shard_map/ppermute | solution.py:20
  7.5 0.9 %collective-permute-start = (bf16[128,512]{1,0:T(8,128)(2,1)S(1)}, bf16[128,512]{1,0:T(8,128)(2,1)S(1)}, u32[]{:S(2)}, u32[]{:S(2)}) collective-permute-start(bf16[128,512]{1,0:T(8,128)(2,1)S(1)} %shard_map.37.weighted), channel_id=1, source_target_pairs={{0,2},{1,3},{2,4},{3,5},{4,6},{5,7},{6,8},{7,9},{8,10},{9,11},{10,... | collective-permute-start | bytes 393224 | tf_op jit(solution)/shard_map/ppermute | solution.py:20
  8.5 2.0 %shard_map.38.acc = f32[128,2048]{1,0:T(8,128)S(1)} custom-call(bf16[128,512]{1,0:T(8,128)(2,1)S(1)} %shard_map.37.weighted, bf16[4,1,512,2048]{3,2,1,0:T(8,128)(2,1)} %panels.5), custom_call_target="tpu_custom_call" | custom-call | flops 268435456 | bytes 3145728 | tf_op jit(solution)/shard_map/pallas_call | solution.py:131
  10.5 5.5 %collective-permute-done.2.ha = bf16[128,512]{1,0:T(8,128)(2,1)S(1)} collective-permute-done((bf16[128,512]{1,0:T(8,128)(2,1)S(1)}, bf16[128,512]{1,0:T(8,128)(2,1)S(1)}, u32[]{:S(2)}, u32[]{:S(2)}) %collective-permute-start.2) | collective-permute-done | bytes 131104 | tf_op jit(solution)/shard_map/ppermute | solution.py:20
  15.9 2.6 %collective-permute-done.1.hb = bf16[128,512]{1,0:T(8,128)(2,1)S(1)} collective-permute-done((bf16[128,512]{1,0:T(8,128)(2,1)S(1)}, bf16[128,512]{1,0:T(8,128)(2,1)S(1)}, u32[]{:S(2)}, u32[]{:S(2)}) %collective-permute-start.1) | collective-permute-done | bytes 131104 | tf_op jit(solution)/shard_map/ppermute | solution.py:20
  18.6 0.0 collective-permute-done.h2
  18.6 0.0 copy-done
  18.6 0.4 %shard_map.40 = bf16[128,512]{1,0:T(8,128)(2,1)S(1)} custom-call(bf16[128,512]{1,0:T(8,128)(2,1)S(1)} %collective-permute-done.h2, bf16[128,512]{1,0:T(8,128)(2,1)S(1)} %collective-permute-done.1.hb, bf16[128,512]{1,0:T(8,128)(2,1)S(1)} %collective-permute-done.2.ha, bf16[4,1,512,2048]{3,2,1,0:T(8,128)(2,1)S(1)} %copy-done, f32[128,2048]{1,0:T(8,128)S(1)} %shard_map.38.acc), custom_call_target="tpu_custom_call" | custom-call | flops 201326592 | bytes 2097152 | tf_op jit(solution)/shard_map/pallas_call | solution.py:141
  19.0 2.5 %collective-permute-start.4 = (bf16[128,512]{1,0:T(8,128)(2,1)S(1)}, bf16[128,512]{1,0:T(8,128)(2,1)S(1)}, u32[]{:S(2)}, u32[]{:S(2)}) collective-permute-start(bf16[128,512]{1,0:T(8,128)(2,1)S(1)} %shard_map.40), channel_id=1, source_target_pairs={{0,64},{64,0},{128,192},{192,128},{1,65},{65,1},{129,193},{193,129... | collective-permute-start | bytes 393224 | tf_op jit(solution)/shard_map/ppermute | solution.py:25
  21.4 0.8 %shard_map.39 = (bf16[128,512]{1,0:T(8,128)(2,1)S(1)}, f32[2,128,512]{2,1,0:T(8,128)S(1)}) custom-call(bf16[128,512]{1,0:T(8,128)(2,1)S(1)} %collective-permute-done.h2, bf16[128,512]{1,0:T(8,128)(2,1)S(1)} %collective-permute-done.1.hb, bf16[128,512]{1,0:T(8,128)(2,1)S(1)} %collective-permute-done.2.ha, bf16[4,1,512,2048]{3,2,1,0:T(8,128)(2,1)S(1)} %copy-done, ...), custom_call_target="tpu_custom_call" | custom-call | flops 603979776 | bytes 6291456 | tf_op jit(solution)/shard_map/pallas_call | solution.py:145
  22.2 0.1 collective-permute-start.3
  22.4 0.1 collective-permute-done.4.other
  22.5 0.5 %collective-permute-start.5 = (bf16[128,512]{1,0:T(8,128)(2,1)S(1)}, bf16[128,512]{1,0:T(8,128)(2,1)S(1)}, u32[]{:S(2)}, u32[]{:S(2)}) collective-permute-start(bf16[128,512]{1,0:T(8,128)(2,1)S(1)} %shard_map.41), channel_id=1, source_target_pairs={{0,128},{64,192},{128,0},{192,64},{1,129},{65,193},{129,1},{193,65... | collective-permute-start | bytes 393224 | tf_op jit(solution)/shard_map/ppermute | solution.py:25
  22.9 0.7 %collective-permute-done.3.other = bf16[128,512]{1,0:T(8,128)(2,1)S(1)} collective-permute-done((bf16[128,512]{1,0:T(8,128)(2,1)S(1)}, bf16[128,512]{1,0:T(8,128)(2,1)S(1)}, u32[]{:S(2)}, u32[]{:S(2)}) %collective-permute-start.3) | collective-permute-done | bytes 131104 | tf_op jit(solution)/shard_map/ppermute | solution.py:25
  23.7 3.5 %collective-permute-done.5.third = bf16[128,512]{1,0:T(8,128)(2,1)S(1)} collective-permute-done((bf16[128,512]{1,0:T(8,128)(2,1)S(1)}, bf16[128,512]{1,0:T(8,128)(2,1)S(1)}, u32[]{:S(2)}, u32[]{:S(2)}) %collective-permute-start.5) | collective-permute-done | bytes 131104 | tf_op jit(solution)/shard_map/ppermute | solution.py:25
  27.2 0.8 %shard_map.42 = f32[512,128]{1,0:T(8,128)} custom-call(f32[2,128,512]{2,1,0:T(8,128)S(1)} %get-tuple-element.7.mine, bf16[128,512]{1,0:T(8,128)(2,1)S(1)} %collective-permute-done.3.other, bf16[128,512]{1,0:T(8,128)(2,1)S(1)} %collective-permute-done.5.third), custom_call_target="tpu_custom_call" | custom-call | bytes 1048576 | tf_op jit(solution)/shard_map/pallas_call | solution.py:157
  (1 shorter events, 0.0 us)
Async XLA Ops:
  1.2 17.4 %copy-start = (bf16[4,1,512,2048]{3,2,1,0:T(8,128)(2,1)S(1)}, bf16[4,1,512,2048]{3,2,1,0:T(8,128)(2,1)}, u32[]{:S(2)}) copy-start(bf16[4,1,512,2048]{3,2,1,0:T(8,128)(2,1)} %panels.5) | copy-start | bytes 25165828
  1.2 14.8 %collective-permute-start.2 = (bf16[128,512]{1,0:T(8,128)(2,1)S(1)}, bf16[128,512]{1,0:T(8,128)(2,1)S(1)}, u32[]{:S(2)}, u32[]{:S(2)}) collective-permute-start(bf16[128,512]{1,0:T(8,128)(2,1)S(1)} %shard_map.37.weighted), channel_id=1, source_target_pairs={{0,1},{1,4},{2,3},{3,6},{4,5},{5,8},{6,7},{7,10},{8,9},{9,12},{10,... | collective-permute-start | bytes 393224 | tf_op jit(solution)/shard_map/ppermute | solution.py:20
  5.0 13.6 %collective-permute-start.1 = (bf16[128,512]{1,0:T(8,128)(2,1)S(1)}, bf16[128,512]{1,0:T(8,128)(2,1)S(1)}, u32[]{:S(2)}, u32[]{:S(2)}) collective-permute-start(bf16[128,512]{1,0:T(8,128)(2,1)S(1)} %shard_map.37.weighted), channel_id=1, source_target_pairs={{0,3},{1,2},{2,5},{3,4},{4,7},{5,6},{6,9},{7,8},{8,11},{9,10},{10,... | collective-permute-start | bytes 393224 | tf_op jit(solution)/shard_map/ppermute | solution.py:20
  7.5 11.0 %collective-permute-start = (bf16[128,512]{1,0:T(8,128)(2,1)S(1)}, bf16[128,512]{1,0:T(8,128)(2,1)S(1)}, u32[]{:S(2)}, u32[]{:S(2)}) collective-permute-start(bf16[128,512]{1,0:T(8,128)(2,1)S(1)} %shard_map.37.weighted), channel_id=1, source_target_pairs={{0,2},{1,3},{2,4},{3,5},{4,6},{5,7},{6,8},{7,9},{8,10},{9,11},{10,... | collective-permute-start | bytes 393224 | tf_op jit(solution)/shard_map/ppermute | solution.py:20
  19.0 3.5 %collective-permute-start.4 = (bf16[128,512]{1,0:T(8,128)(2,1)S(1)}, bf16[128,512]{1,0:T(8,128)(2,1)S(1)}, u32[]{:S(2)}, u32[]{:S(2)}) collective-permute-start(bf16[128,512]{1,0:T(8,128)(2,1)S(1)} %shard_map.40), channel_id=1, source_target_pairs={{0,64},{64,0},{128,192},{192,128},{1,65},{65,1},{129,193},{193,129... | collective-permute-start | bytes 393224 | tf_op jit(solution)/shard_map/ppermute | solution.py:25
  22.2 1.4 %collective-permute-start.3 = (bf16[128,512]{1,0:T(8,128)(2,1)S(1)}, bf16[128,512]{1,0:T(8,128)(2,1)S(1)}, u32[]{:S(2)}, u32[]{:S(2)}) collective-permute-start(bf16[128,512]{1,0:T(8,128)(2,1)S(1)} %get-tuple-element.8), channel_id=1, source_target_pairs={{0,64},{64,0},{128,192},{192,128},{1,65},{65,1},{129,193},{193,129... | collective-permute-start | bytes 393224 | tf_op jit(solution)/shard_map/ppermute | solution.py:25
  22.5 4.7 %collective-permute-start.5 = (bf16[128,512]{1,0:T(8,128)(2,1)S(1)}, bf16[128,512]{1,0:T(8,128)(2,1)S(1)}, u32[]{:S(2)}, u32[]{:S(2)}) collective-permute-start(bf16[128,512]{1,0:T(8,128)(2,1)S(1)} %shard_map.41), channel_id=1, source_target_pairs={{0,128},{64,192},{128,0},{192,64},{1,129},{65,193},{129,1},{193,65... | collective-permute-start | bytes 393224 | tf_op jit(solution)/shard_map/ppermute | solution.py:25

commit v2 on v1

--- a/solution.py
+++ b/solution.py
@@ -5,6 +5,8 @@
 from jax.experimental.pallas import tpu as pltpu
 from jax.sharding import PartitionSpec as P
 
+
+SHIFTS = ((3, 1), (1, 3), (2, 2))
 
 VMEM = pl.BlockSpec(memory_space=pltpu.VMEM)
 HBM = pl.BlockSpec(memory_space=pltpu.HBM)
@@ -75,20 +77,21 @@
     where = pl.ds(pl.multiple_of(band * cells, cells), cells)
     odd = lax.axis_index("lon") % 2
     total = acc[:, where]
-    for d, h in zip((3 - 2 * odd, 1 + 2 * odd, 2), halo):
+    for (from_even, from_odd), h in zip(SHIFTS, halo):
+        d = from_odd + (from_even - from_odd) * odd
         total += jnp.dot(h[...], panels[d, 0, :, where], preferred_element_type=jnp.float32)
     return total
 
 
-def far_body(h2, hb, ha, panels, acc, out):
+def far_body(ha, hb, hc, panels, acc, out):
     band = 3 - lax.axis_index("lat")
-    out[...] = band_sum((ha, hb, h2), panels, acc, band, h2.shape[1]).astype(out.dtype)
+    out[...] = band_sum((ha, hb, hc), panels, acc, band, ha.shape[1]).astype(out.dtype)
 
 
-def rest_body(h2, hb, ha, panels, acc, near, mine):
+def rest_body(ha, hb, hc, panels, acc, near, mine):
     band = lax.axis_index("lat")
     partner = band + 1 - 2 * (band % 2)
-    halo, cells = (ha, hb, h2), h2.shape[1]
+    halo, cells = (ha, hb, hc), ha.shape[1]
     near[...] = band_sum(halo, panels, acc, partner, cells).astype(near.dtype)
     mine[0] = band_sum(halo, panels, acc, 3 - partner, cells)
     mine[1] = band_sum(halo, panels, acc, band, cells)
@@ -124,9 +127,10 @@
         MB // 4,
         58 * MB,
     )(in_hbm(residual), in_hbm(noise_weights.T))
-    ha = eastward(weighted, 1, 3)
-    hb = eastward(weighted, 3, 1)
-    h2 = eastward(weighted, 2, 2)
+    halo = []
+    for shifts in SHIFTS:
+        halo.append(eastward(weighted, *shifts))
+    ha, hb, hc = halo
     flops = 2 * probes * cells * every
     acc = call(
         first_body,
@@ -139,7 +143,7 @@
     )(weighted, in_hbm(kernel))
     flops = 6 * probes * cells * cells
     far = call(far_body, shape((probes, cells), bf16), [VMEM] * 5, [], flops, 2 * MB, 8 * MB)(
-        h2, hb, ha, kernel, acc
+        ha, hb, hc, kernel, acc
     )
     other_far = swapped(far, 1)
     near, mine = call(
@@ -150,7 +154,7 @@
         3 * flops,
         6 * MB,
         8 * MB,
-    )(h2, hb, ha, kernel, acc)
+    )(ha, hb, hc, kernel, acc)
     packed = call(pack_body, shape((probes, cells), bf16), [VMEM] * 2, [], 0, MB, 4 * MB)(mine, other_far)
     third = swapped(packed, 2)
     other_near = swapped(near, 1)

time: 28.1 us -> 29.7 us (1.057)
  waiting for transfers between devices: 12.4 us -> 14.5 us
  starting transfers between devices: 10.4 us -> 9.83 us
    ppermute x3, waiting for transfers between devices: 8.07 us -> 10.2 us  [eastward(): return lax.ppermute(value, 'lon', pairs)]
    ppermute x3, starting transfers between devices: 3.08 us -> 1.92 us  [swapped(): return lax.ppermute(value, 'lat', [(i, i ^ mask) for i in range(length)])]
    ppermute x3, starting transfers between devices: 7.3 us -> 7.91 us  [eastward(): return lax.ppermute(value, 'lon', pairs)]
  transfers between devices with their start and end apart: 6 -> 6, of which waited for: 5 -> 6; matrix products, arithmetic and copies ran while one was open for 0% -> 0% of each run, Pallas kernels for 10% -> 10%
where the time goes in v2:
time: 29.7 us; the launch traced here: 29.6 us
  waiting for transfers between devices  14.5 us (49%)
  starting transfers between devices  9.83 us (33%)
  Pallas kernels  5.21 us (18%)
    ppermute x3, waiting for transfers between devices, eastward(): return lax.ppermute(value, 'lon', pairs)  10.2 us
    ppermute x3, starting transfers between devices, eastward(): return lax.ppermute(value, 'lon', pairs)  7.91 us
    ppermute x3, waiting for transfers between devices, swapped(): return lax.ppermute(value, 'lat', [(i, i ^ mask) for i in range(length)])  4.32 us
    pallas_call x1, Pallas kernels, sweep(): call(first_body, shape((probes, every), f32), [VMEM, HBM], [pltpu.VMEM((c...  2 us
    ppermute x3, starting transfers between devices, swapped(): return lax.ppermute(value, 'lat', [(i, i ^ mask) for i in range(length)])  1.92 us
    pallas_call x1, Pallas kernels, sweep(): call(weigh_body, pltpu.VMEM((probes, cells), bf16), [HBM] * 2, [pltpu.VME...  1.16 us
    pallas_call x1, Pallas kernels, sweep(): call(final_body, shape((cells, probes), f32), [VMEM] * 3, [], 0, MB, 4 * MB)  0.84 us
    pallas_call x1, Pallas kernels, sweep(): call(rest_body, (shape((probes, cells), bf16), shape((2, probes, cells),...  0.8 us
  transfers between devices with their start and end apart: 6, of which 6 were waited for; matrix products, arithmetic and copies ran while one was open for 0% of the time, Pallas kernels for 10%

profile of v2, /device:TPU:1, one launch (start us, length us, event | category | flops | bytes accessed | tf_op | source)
XLA Modules:
  0.0 29.6 jit_solution(15131172229362453405)
XLA Ops:
  0.0 1.2 %shard_map.37.weighted = bf16[128,512]{1,0:T(8,128)(2,1)S(1)} custom-call(bf16[32,16,128]{2,1,0:T(8,128)(2,1)} %residual.1, f32[16,32]{1,0:T(8,128)} %bitcast.2), custom_call_target="tpu_custom_call" | custom-call | bytes 262144 | tf_op jit(solution)/shard_map/pallas_call | solution.py:117
  1.2 0.0 copy-start
  1.2 2.1 %collective-permute-start.2 = (bf16[128,512]{1,0:T(8,128)(2,1)S(1)}, bf16[128,512]{1,0:T(8,128)(2,1)S(1)}, u32[]{:S(2)}, u32[]{:S(2)}) collective-permute-start(bf16[128,512]{1,0:T(8,128)(2,1)S(1)} %shard_map.37.weighted), channel_id=1, source_target_pairs={{0,2},{1,3},{2,4},{3,5},{4,6},{5,7},{6,8},{7,9},{8,10},{9,11},{10,... | collective-permute-start | bytes 393224 | tf_op jit(solution)/shard_map/ppermute | solution.py:22
  3.3 2.9 %collective-permute-start.1 = (bf16[128,512]{1,0:T(8,128)(2,1)S(1)}, bf16[128,512]{1,0:T(8,128)(2,1)S(1)}, u32[]{:S(2)}, u32[]{:S(2)}) collective-permute-start(bf16[128,512]{1,0:T(8,128)(2,1)S(1)} %shard_map.37.weighted), channel_id=1, source_target_pairs={{0,1},{1,4},{2,3},{3,6},{4,5},{5,8},{6,7},{7,10},{8,9},{9,12},{10,... | collective-permute-start | bytes 393224 | tf_op jit(solution)/shard_map/ppermute | solution.py:22
  6.2 2.9 %collective-permute-start = (bf16[128,512]{1,0:T(8,128)(2,1)S(1)}, bf16[128,512]{1,0:T(8,128)(2,1)S(1)}, u32[]{:S(2)}, u32[]{:S(2)}) collective-permute-start(bf16[128,512]{1,0:T(8,128)(2,1)S(1)} %shard_map.37.weighted), channel_id=1, source_target_pairs={{0,3},{1,2},{2,5},{3,4},{4,7},{5,6},{6,9},{7,8},{8,11},{9,10},{10,... | collective-permute-start | bytes 393224 | tf_op jit(solution)/shard_map/ppermute | solution.py:22
  9.1 2.0 %shard_map.38.acc = f32[128,2048]{1,0:T(8,128)S(1)} custom-call(bf16[128,512]{1,0:T(8,128)(2,1)S(1)} %shard_map.37.weighted, bf16[4,1,512,2048]{3,2,1,0:T(8,128)(2,1)} %panels.5), custom_call_target="tpu_custom_call" | custom-call | flops 268435456 | bytes 3145728 | tf_op jit(solution)/shard_map/pallas_call | solution.py:135
  11.1 1.9 %collective-permute-done.2.hc = bf16[128,512]{1,0:T(8,128)(2,1)S(1)} collective-permute-done((bf16[128,512]{1,0:T(8,128)(2,1)S(1)}, bf16[128,512]{1,0:T(8,128)(2,1)S(1)}, u32[]{:S(2)}, u32[]{:S(2)}) %collective-permute-start.2) | collective-permute-done | bytes 131104 | tf_op jit(solution)/shard_map/ppermute | solution.py:22
  13.1 4.6 %collective-permute-done.1.hb = bf16[128,512]{1,0:T(8,128)(2,1)S(1)} collective-permute-done((bf16[128,512]{1,0:T(8,128)(2,1)S(1)}, bf16[128,512]{1,0:T(8,128)(2,1)S(1)}, u32[]{:S(2)}, u32[]{:S(2)}) %collective-permute-start.1) | collective-permute-done | bytes 131104 | tf_op jit(solution)/shard_map/ppermute | solution.py:22
  17.7 3.6 %collective-permute-done.ha = bf16[128,512]{1,0:T(8,128)(2,1)S(1)} collective-permute-done((bf16[128,512]{1,0:T(8,128)(2,1)S(1)}, bf16[128,512]{1,0:T(8,128)(2,1)S(1)}, u32[]{:S(2)}, u32[]{:S(2)}) %collective-permute-start) | collective-permute-done | bytes 131104 | tf_op jit(solution)/shard_map/ppermute | solution.py:22
  21.3 0.0 copy-done
  21.3 0.4 %shard_map.40 = bf16[128,512]{1,0:T(8,128)(2,1)S(1)} custom-call(bf16[128,512]{1,0:T(8,128)(2,1)S(1)} %collective-permute-done.ha, bf16[128,512]{1,0:T(8,128)(2,1)S(1)} %collective-permute-done.1.hb, bf16[128,512]{1,0:T(8,128)(2,1)S(1)} %collective-permute-done.2.hc, bf16[4,1,512,2048]{3,2,1,0:T(8,128)(2,1)S(1)} %copy-done, f32[128,2048]{1,0:T(8,128)S(1)} %shard_map.38.acc), custom_call_target="tpu_custom_call" | custom-call | flops 201326592 | bytes 2097152 | tf_op jit(solution)/shard_map/pallas_call | solution.py:145
  21.7 1.3 %collective-permute-start.4 = (bf16[128,512]{1,0:T(8,128)(2,1)S(1)}, bf16[128,512]{1,0:T(8,128)(2,1)S(1)}, u32[]{:S(2)}, u32[]{:S(2)}) collective-permute-start(bf16[128,512]{1,0:T(8,128)(2,1)S(1)} %shard_map.40), channel_id=1, source_target_pairs={{0,64},{64,0},{128,192},{192,128},{1,65},{65,1},{129,193},{193,129... | collective-permute-start | bytes 393224 | tf_op jit(solution)/shard_map/ppermute | solution.py:27
  23.0 0.8 %shard_map.39 = (bf16[128,512]{1,0:T(8,128)(2,1)S(1)}, f32[2,128,512]{2,1,0:T(8,128)S(1)}) custom-call(bf16[128,512]{1,0:T(8,128)(2,1)S(1)} %collective-permute-done.ha, bf16[128,512]{1,0:T(8,128)(2,1)S(1)} %collective-permute-done.1.hb, bf16[128,512]{1,0:T(8,128)(2,1)S(1)} %collective-permute-done.2.hc, bf16[4,1,512,2048]{3,2,1,0:T(8,128)(2,1)S(1)} %copy-done, ...), custom_call_target="tpu_custom_call" | custom-call | flops 603979776 | bytes 6291456 | tf_op jit(solution)/shard_map/pallas_call | solution.py:149
  23.8 0.1 collective-permute-start.3
  23.9 0.1 collective-permute-done.4.other
  24.0 0.5 %collective-permute-start.5 = (bf16[128,512]{1,0:T(8,128)(2,1)S(1)}, bf16[128,512]{1,0:T(8,128)(2,1)S(1)}, u32[]{:S(2)}, u32[]{:S(2)}) collective-permute-start(bf16[128,512]{1,0:T(8,128)(2,1)S(1)} %shard_map.41), channel_id=1, source_target_pairs={{0,128},{64,192},{128,0},{192,64},{1,129},{65,193},{129,1},{193,65... | collective-permute-start | bytes 393224 | tf_op jit(solution)/shard_map/ppermute | solution.py:27
  24.5 0.7 %collective-permute-done.3.other = bf16[128,512]{1,0:T(8,128)(2,1)S(1)} collective-permute-done((bf16[128,512]{1,0:T(8,128)(2,1)S(1)}, bf16[128,512]{1,0:T(8,128)(2,1)S(1)}, u32[]{:S(2)}, u32[]{:S(2)}) %collective-permute-start.3) | collective-permute-done | bytes 131104 | tf_op jit(solution)/shard_map/ppermute | solution.py:27
  25.3 3.5 %collective-permute-done.5.third = bf16[128,512]{1,0:T(8,128)(2,1)S(1)} collective-permute-done((bf16[128,512]{1,0:T(8,128)(2,1)S(1)}, bf16[128,512]{1,0:T(8,128)(2,1)S(1)}, u32[]{:S(2)}, u32[]{:S(2)}) %collective-permute-start.5) | collective-permute-done | bytes 131104 | tf_op jit(solution)/shard_map/ppermute | solution.py:27
  28.8 0.8 %shard_map.42 = f32[512,128]{1,0:T(8,128)} custom-call(f32[2,128,512]{2,1,0:T(8,128)S(1)} %get-tuple-element.7.mine, bf16[128,512]{1,0:T(8,128)(2,1)S(1)} %collective-permute-done.3.other, bf16[128,512]{1,0:T(8,128)(2,1)S(1)} %collective-permute-done.5.third), custom_call_target="tpu_custom_call" | custom-call | bytes 1048576 | tf_op jit(solution)/shard_map/pallas_call | solution.py:161
  (1 shorter events, 0.0 us)
Async XLA Ops:
  1.2 20.1 %copy-start = (bf16[4,1,512,2048]{3,2,1,0:T(8,128)(2,1)S(1)}, bf16[4,1,512,2048]{3,2,1,0:T(8,128)(2,1)}, u32[]{:S(2)}) copy-start(bf16[4,1,512,2048]{3,2,1,0:T(8,128)(2,1)} %panels.5) | copy-start | bytes 25165828
  1.2 11.9 %collective-permute-start.2 = (bf16[128,512]{1,0:T(8,128)(2,1)S(1)}, bf16[128,512]{1,0:T(8,128)(2,1)S(1)}, u32[]{:S(2)}, u32[]{:S(2)}) collective-permute-start(bf16[128,512]{1,0:T(8,128)(2,1)S(1)} %shard_map.37.weighted), channel_id=1, source_target_pairs={{0,2},{1,3},{2,4},{3,5},{4,6},{5,7},{6,8},{7,9},{8,10},{9,11},{10,... | collective-permute-start | bytes 393224 | tf_op jit(solution)/shard_map/ppermute | solution.py:22
  3.3 14.4 %collective-permute-start.1 = (bf16[128,512]{1,0:T(8,128)(2,1)S(1)}, bf16[128,512]{1,0:T(8,128)(2,1)S(1)}, u32[]{:S(2)}, u32[]{:S(2)}) collective-permute-start(bf16[128,512]{1,0:T(8,128)(2,1)S(1)} %shard_map.37.weighted), channel_id=1, source_target_pairs={{0,1},{1,4},{2,3},{3,6},{4,5},{5,8},{6,7},{7,10},{8,9},{9,12},{10,... | collective-permute-start | bytes 393224 | tf_op jit(solution)/shard_map/ppermute | solution.py:22
  6.2 15.1 %collective-permute-start = (bf16[128,512]{1,0:T(8,128)(2,1)S(1)}, bf16[128,512]{1,0:T(8,128)(2,1)S(1)}, u32[]{:S(2)}, u32[]{:S(2)}) collective-permute-start(bf16[128,512]{1,0:T(8,128)(2,1)S(1)} %shard_map.37.weighted), channel_id=1, source_target_pairs={{0,3},{1,2},{2,5},{3,4},{4,7},{5,6},{6,9},{7,8},{8,11},{9,10},{10,... | collective-permute-start | bytes 393224 | tf_op jit(solution)/shard_map/ppermute | solution.py:22
  21.7 2.3 %collective-permute-start.4 = (bf16[128,512]{1,0:T(8,128)(2,1)S(1)}, bf16[128,512]{1,0:T(8,128)(2,1)S(1)}, u32[]{:S(2)}, u32[]{:S(2)}) collective-permute-start(bf16[128,512]{1,0:T(8,128)(2,1)S(1)} %shard_map.40), channel_id=1, source_target_pairs={{0,64},{64,0},{128,192},{192,128},{1,65},{65,1},{129,193},{193,129... | collective-permute-start | bytes 393224 | tf_op jit(solution)/shard_map/ppermute | solution.py:27
  23.8 1.4 %collective-permute-start.3 = (bf16[128,512]{1,0:T(8,128)(2,1)S(1)}, bf16[128,512]{1,0:T(8,128)(2,1)S(1)}, u32[]{:S(2)}, u32[]{:S(2)}) collective-permute-start(bf16[128,512]{1,0:T(8,128)(2,1)S(1)} %get-tuple-element.8), channel_id=1, source_target_pairs={{0,64},{64,0},{128,192},{192,128},{1,65},{65,1},{129,193},{193,129... | collective-permute-start | bytes 393224 | tf_op jit(solution)/shard_map/ppermute | solution.py:27
  24.0 4.7 %collective-permute-start.5 = (bf16[128,512]{1,0:T(8,128)(2,1)S(1)}, bf16[128,512]{1,0:T(8,128)(2,1)S(1)}, u32[]{:S(2)}, u32[]{:S(2)}) collective-permute-start(bf16[128,512]{1,0:T(8,128)(2,1)S(1)} %shard_map.41), channel_id=1, source_target_pairs={{0,128},{64,192},{128,0},{192,64},{1,129},{65,193},{129,1},{193,65... | collective-permute-start | bytes 393224 | tf_op jit(solution)/shard_map/ppermute | solution.py:27

commit v3 on v2

--- a/solution.py
+++ b/solution.py
@@ -55,22 +55,19 @@
     out[...] = jnp.concatenate(part, axis=0).T
 
 
-def first_body(weighted, panels, acc, own, sems):
+def first_body(weighted, panels, acc, staged, own, sems):
     cells = weighted.shape[1]
-    depth = cells // sems.shape[0]
-    copies = [
-        pltpu.make_async_copy(
-            panels.at[0, 0, pl.ds(i * depth, depth)], own.at[pl.ds(i * depth, depth)], sems.at[i]
-        )
-        for i in range(sems.shape[0])
-    ]
+    copies = [pltpu.make_async_copy(panels.at[0, 0], own, sems.at[0])]
+    for d in range(1, 4):
+        copies.append(pltpu.make_async_copy(panels.at[d, 0], staged.at[d - 1], sems.at[d]))
     for copy in copies:
         copy.start()
-    for copy in copies:
-        copy.wait()
+    copies[0].wait()
     for k in range(panels.shape[3] // cells):
         where = slice(k * cells, (k + 1) * cells)
         acc[:, where] = jnp.dot(weighted[...], own[:, where], preferred_element_type=jnp.float32)
+    for copy in copies[1:]:
+        copy.wait()
 
 
 def band_sum(halo, panels, acc, band, cells):
@@ -79,7 +76,7 @@
     total = acc[:, where]
     for (from_even, from_odd), h in zip(SHIFTS, halo):
         d = from_odd + (from_even - from_odd) * odd
-        total += jnp.dot(h[...], panels[d, 0, :, where], preferred_element_type=jnp.float32)
+        total += jnp.dot(h[...], panels[d - 1, :, where], preferred_element_type=jnp.float32)
     return total
 
 
@@ -132,18 +129,18 @@
         halo.append(eastward(weighted, *shifts))
     ha, hb, hc = halo
     flops = 2 * probes * cells * every
-    acc = call(
+    acc, staged = call(
         first_body,
-        shape((probes, every), f32),
+        (shape((probes, every), f32), shape((3, cells, every), bf16)),
         [VMEM, HBM],
         [pltpu.VMEM((cells, every), bf16), pltpu.SemaphoreType.DMA((4,))],
         flops,
-        3 * MB,
-        8 * MB,
+        9 * MB,
+        16 * MB,
     )(weighted, in_hbm(kernel))
     flops = 6 * probes * cells * cells
     far = call(far_body, shape((probes, cells), bf16), [VMEM] * 5, [], flops, 2 * MB, 8 * MB)(
-        ha, hb, hc, kernel, acc
+        ha, hb, hc, staged, acc
     )
     other_far = swapped(far, 1)
     near, mine = call(
@@ -154,7 +151,7 @@
         3 * flops,
         6 * MB,
         8 * MB,
-    )(ha, hb, hc, kernel, acc)
+    )(ha, hb, hc, staged, acc)
     packed = call(pack_body, shape((probes, cells), bf16), [VMEM] * 2, [], 0, MB, 4 * MB)(mine, other_far)
     third = swapped(packed, 2)
     other_near = swapped(near, 1)

time: 29.7 us -> 29.7 us (level)
  waiting for transfers between devices: 14.5 us -> 13 us
  Pallas kernels: 5.21 us -> 6.7 us
    pallas_call x1, Pallas kernels: 2 us -> 3.5 us  [sweep(): call(first_body, (shape((probes, every), f32), shape((3, cells, every), b...]
    ppermute x3, waiting for transfers between devices: 10.2 us -> 8.7 us  [eastward(): return lax.ppermute(value, 'lon', pairs)]
  transfers between devices with their start and end apart: 6 -> 6, of which waited for: 6 -> 6; matrix products, arithmetic and copies ran while one was open for 0% -> 0% of each run, Pallas kernels for 10% -> 15%
where the time goes in v3:
time: 29.7 us; the launch traced here: 29.6 us
  waiting for transfers between devices  13 us (44%)
  starting transfers between devices  9.84 us (33%)
  Pallas kernels  6.7 us (23%)
    ppermute x3, waiting for transfers between devices, eastward(): return lax.ppermute(value, 'lon', pairs)  8.7 us
    ppermute x3, starting transfers between devices, eastward(): return lax.ppermute(value, 'lon', pairs)  7.91 us
    ppermute x3, waiting for transfers between devices, swapped(): return lax.ppermute(value, 'lat', [(i, i ^ mask) for i in range(length)])  4.32 us
    pallas_call x1, Pallas kernels, sweep(): call(first_body, (shape((probes, every), f32), shape((3, cells, every), b...  3.5 us
    ppermute x3, starting transfers between devices, swapped(): return lax.ppermute(value, 'lat', [(i, i ^ mask) for i in range(length)])  1.94 us
    pallas_call x1, Pallas kernels, sweep(): call(weigh_body, pltpu.VMEM((probes, cells), bf16), [HBM] * 2, [pltpu.VME...  1.16 us
    pallas_call x1, Pallas kernels, sweep(): call(final_body, shape((cells, probes), f32), [VMEM] * 3, [], 0, MB, 4 * MB)  0.84 us
    pallas_call x1, Pallas kernels, sweep(): call(rest_body, (shape((probes, cells), bf16), shape((2, probes, cells),...  0.79 us
  transfers between devices with their start and end apart: 6, of which 6 were waited for; matrix products, arithmetic and copies ran while one was open for 0% of the time, Pallas kernels for 15%

profile of v3, /device:TPU:1, one launch (start us, length us, event | category | flops | bytes accessed | tf_op | source)
XLA Modules:
  0.0 29.6 jit_solution(7461954479339685363)
XLA Ops:
  0.0 1.2 %shard_map.37.weighted = bf16[128,512]{1,0:T(8,128)(2,1)S(1)} custom-call(bf16[32,16,128]{2,1,0:T(8,128)(2,1)} %residual.1, f32[16,32]{1,0:T(8,128)} %bitcast.2), custom_call_target="tpu_custom_call" | custom-call | bytes 262144 | tf_op jit(solution)/shard_map/pallas_call | solution.py:114
  1.2 2.1 %collective-permute-start.2 = (bf16[128,512]{1,0:T(8,128)(2,1)S(1)}, bf16[128,512]{1,0:T(8,128)(2,1)S(1)}, u32[]{:S(2)}, u32[]{:S(2)}) collective-permute-start(bf16[128,512]{1,0:T(8,128)(2,1)S(1)} %shard_map.37.weighted), channel_id=1, source_target_pairs={{0,2},{1,3},{2,4},{3,5},{4,6},{5,7},{6,8},{7,9},{8,10},{9,11},{10,... | collective-permute-start | bytes 393224 | tf_op jit(solution)/shard_map/ppermute | solution.py:22
  3.3 2.9 %collective-permute-start.1 = (bf16[128,512]{1,0:T(8,128)(2,1)S(1)}, bf16[128,512]{1,0:T(8,128)(2,1)S(1)}, u32[]{:S(2)}, u32[]{:S(2)}) collective-permute-start(bf16[128,512]{1,0:T(8,128)(2,1)S(1)} %shard_map.37.weighted), channel_id=1, source_target_pairs={{0,1},{1,4},{2,3},{3,6},{4,5},{5,8},{6,7},{7,10},{8,9},{9,12},{10,... | collective-permute-start | bytes 393224 | tf_op jit(solution)/shard_map/ppermute | solution.py:22
  6.2 2.9 %collective-permute-start = (bf16[128,512]{1,0:T(8,128)(2,1)S(1)}, bf16[128,512]{1,0:T(8,128)(2,1)S(1)}, u32[]{:S(2)}, u32[]{:S(2)}) collective-permute-start(bf16[128,512]{1,0:T(8,128)(2,1)S(1)} %shard_map.37.weighted), channel_id=1, source_target_pairs={{0,3},{1,2},{2,5},{3,4},{4,7},{5,6},{6,9},{7,8},{8,11},{9,10},{10,... | collective-permute-start | bytes 393224 | tf_op jit(solution)/shard_map/ppermute | solution.py:22
  9.1 3.5 %shard_map.38 = (f32[128,2048]{1,0:T(8,128)S(1)}, bf16[3,512,2048]{2,1,0:T(8,128)(2,1)S(1)}) custom-call(bf16[128,512]{1,0:T(8,128)(2,1)S(1)} %shard_map.37.weighted, bf16[4,1,512,2048]{3,2,1,0:T(8,128)(2,1)} %panels.1), custom_call_target="tpu_custom_call" | custom-call | flops 268435456 | bytes 9437184 | tf_op jit(solution)/shard_map/pallas_call | solution.py:132
  12.6 0.5 %collective-permute-done.2.hc = bf16[128,512]{1,0:T(8,128)(2,1)S(1)} collective-permute-done((bf16[128,512]{1,0:T(8,128)(2,1)S(1)}, bf16[128,512]{1,0:T(8,128)(2,1)S(1)}, u32[]{:S(2)}, u32[]{:S(2)}) %collective-permute-start.2) | collective-permute-done | bytes 131104 | tf_op jit(solution)/shard_map/ppermute | solution.py:22
  13.0 4.6 %collective-permute-done.1.hb = bf16[128,512]{1,0:T(8,128)(2,1)S(1)} collective-permute-done((bf16[128,512]{1,0:T(8,128)(2,1)S(1)}, bf16[128,512]{1,0:T(8,128)(2,1)S(1)}, u32[]{:S(2)}, u32[]{:S(2)}) %collective-permute-start.1) | collective-permute-done | bytes 131104 | tf_op jit(solution)/shard_map/ppermute | solution.py:22
  17.7 3.6 %collective-permute-done.ha = bf16[128,512]{1,0:T(8,128)(2,1)S(1)} collective-permute-done((bf16[128,512]{1,0:T(8,128)(2,1)S(1)}, bf16[128,512]{1,0:T(8,128)(2,1)S(1)}, u32[]{:S(2)}, u32[]{:S(2)}) %collective-permute-start) | collective-permute-done | bytes 131104 | tf_op jit(solution)/shard_map/ppermute | solution.py:22
  21.3 0.4 %shard_map.40 = bf16[128,512]{1,0:T(8,128)(2,1)S(1)} custom-call(bf16[128,512]{1,0:T(8,128)(2,1)S(1)} %collective-permute-done.ha, bf16[128,512]{1,0:T(8,128)(2,1)S(1)} %collective-permute-done.1.hb, bf16[128,512]{1,0:T(8,128)(2,1)S(1)} %collective-permute-done.2.hc, bf16[3,512,2048]{2,1,0:T(8,128)(2,1)S(1)} %get-tuple-element.9.panels, ...), custom_call_target="tpu_custom_call" | custom-call | flops 201326592 | bytes 2097152 | tf_op jit(solution)/shard_map/pallas_call | solution.py:142
  21.7 1.3 %collective-permute-start.4 = (bf16[128,512]{1,0:T(8,128)(2,1)S(1)}, bf16[128,512]{1,0:T(8,128)(2,1)S(1)}, u32[]{:S(2)}, u32[]{:S(2)}) collective-permute-start(bf16[128,512]{1,0:T(8,128)(2,1)S(1)} %shard_map.40), channel_id=1, source_target_pairs={{0,64},{64,0},{128,192},{192,128},{1,65},{65,1},{129,193},{193,129... | collective-permute-start | bytes 393224 | tf_op jit(solution)/shard_map/ppermute | solution.py:27
  23.0 0.8 %shard_map.39 = (bf16[128,512]{1,0:T(8,128)(2,1)S(1)}, f32[2,128,512]{2,1,0:T(8,128)S(1)}) custom-call(bf16[128,512]{1,0:T(8,128)(2,1)S(1)} %collective-permute-done.ha, bf16[128,512]{1,0:T(8,128)(2,1)S(1)} %collective-permute-done.1.hb, bf16[128,512]{1,0:T(8,128)(2,1)S(1)} %collective-permute-done.2.hc, bf16[3,512,2048]{2,1,0:T(8,128)(2,1)S(1)} %get-tuple-element.9.panels, ...), custom_call_target="tpu_custom_call" | custom-call | flops 603979776 | bytes 6291456 | tf_op jit(solution)/shard_map/pallas_call | solution.py:146
  23.8 0.1 collective-permute-start.3
  23.9 0.1 collective-permute-done.4.other
  24.0 0.5 %collective-permute-start.5 = (bf16[128,512]{1,0:T(8,128)(2,1)S(1)}, bf16[128,512]{1,0:T(8,128)(2,1)S(1)}, u32[]{:S(2)}, u32[]{:S(2)}) collective-permute-start(bf16[128,512]{1,0:T(8,128)(2,1)S(1)} %shard_map.41), channel_id=1, source_target_pairs={{0,128},{64,192},{128,0},{192,64},{1,129},{65,193},{129,1},{193,65... | collective-permute-start | bytes 393224 | tf_op jit(solution)/shard_map/ppermute | solution.py:27
  24.5 0.7 %collective-permute-done.3.other = bf16[128,512]{1,0:T(8,128)(2,1)S(1)} collective-permute-done((bf16[128,512]{1,0:T(8,128)(2,1)S(1)}, bf16[128,512]{1,0:T(8,128)(2,1)S(1)}, u32[]{:S(2)}, u32[]{:S(2)}) %collective-permute-start.3) | collective-permute-done | bytes 131104 | tf_op jit(solution)/shard_map/ppermute | solution.py:27
  25.2 3.5 %collective-permute-done.5.third = bf16[128,512]{1,0:T(8,128)(2,1)S(1)} collective-permute-done((bf16[128,512]{1,0:T(8,128)(2,1)S(1)}, bf16[128,512]{1,0:T(8,128)(2,1)S(1)}, u32[]{:S(2)}, u32[]{:S(2)}) %collective-permute-start.5) | collective-permute-done | bytes 131104 | tf_op jit(solution)/shard_map/ppermute | solution.py:27
  28.8 0.8 %shard_map.42 = f32[512,128]{1,0:T(8,128)} custom-call(f32[2,128,512]{2,1,0:T(8,128)S(1)} %get-tuple-element.11.mine, bf16[128,512]{1,0:T(8,128)(2,1)S(1)} %collective-permute-done.3.other, bf16[128,512]{1,0:T(8,128)(2,1)S(1)} %collective-permute-done.5.third), custom_call_target="tpu_custom_call" | custom-call | bytes 1048576 | tf_op jit(solution)/shard_map/pallas_call | solution.py:158
  (1 shorter events, 0.0 us)
Async XLA Ops:
  1.2 11.9 %collective-permute-start.2 = (bf16[128,512]{1,0:T(8,128)(2,1)S(1)}, bf16[128,512]{1,0:T(8,128)(2,1)S(1)}, u32[]{:S(2)}, u32[]{:S(2)}) collective-permute-start(bf16[128,512]{1,0:T(8,128)(2,1)S(1)} %shard_map.37.weighted), channel_id=1, source_target_pairs={{0,2},{1,3},{2,4},{3,5},{4,6},{5,7},{6,8},{7,9},{8,10},{9,11},{10,... | collective-permute-start | bytes 393224 | tf_op jit(solution)/shard_map/ppermute | solution.py:22
  3.3 14.4 %collective-permute-start.1 = (bf16[128,512]{1,0:T(8,128)(2,1)S(1)}, bf16[128,512]{1,0:T(8,128)(2,1)S(1)}, u32[]{:S(2)}, u32[]{:S(2)}) collective-permute-start(bf16[128,512]{1,0:T(8,128)(2,1)S(1)} %shard_map.37.weighted), channel_id=1, source_target_pairs={{0,1},{1,4},{2,3},{3,6},{4,5},{5,8},{6,7},{7,10},{8,9},{9,12},{10,... | collective-permute-start | bytes 393224 | tf_op jit(solution)/shard_map/ppermute | solution.py:22
  6.2 15.1 %collective-permute-start = (bf16[128,512]{1,0:T(8,128)(2,1)S(1)}, bf16[128,512]{1,0:T(8,128)(2,1)S(1)}, u32[]{:S(2)}, u32[]{:S(2)}) collective-permute-start(bf16[128,512]{1,0:T(8,128)(2,1)S(1)} %shard_map.37.weighted), channel_id=1, source_target_pairs={{0,3},{1,2},{2,5},{3,4},{4,7},{5,6},{6,9},{7,8},{8,11},{9,10},{10,... | collective-permute-start | bytes 393224 | tf_op jit(solution)/shard_map/ppermute | solution.py:22
  21.7 2.3 %collective-permute-start.4 = (bf16[128,512]{1,0:T(8,128)(2,1)S(1)}, bf16[128,512]{1,0:T(8,128)(2,1)S(1)}, u32[]{:S(2)}, u32[]{:S(2)}) collective-permute-start(bf16[128,512]{1,0:T(8,128)(2,1)S(1)} %shard_map.40), channel_id=1, source_target_pairs={{0,64},{64,0},{128,192},{192,128},{1,65},{65,1},{129,193},{193,129... | collective-permute-start | bytes 393224 | tf_op jit(solution)/shard_map/ppermute | solution.py:27
  23.8 1.4 %collective-permute-start.3 = (bf16[128,512]{1,0:T(8,128)(2,1)S(1)}, bf16[128,512]{1,0:T(8,128)(2,1)S(1)}, u32[]{:S(2)}, u32[]{:S(2)}) collective-permute-start(bf16[128,512]{1,0:T(8,128)(2,1)S(1)} %get-tuple-element.12), channel_id=1, source_target_pairs={{0,64},{64,0},{128,192},{192,128},{1,65},{65,1},{129,193},{193,129... | collective-permute-start | bytes 393224 | tf_op jit(solution)/shard_map/ppermute | solution.py:27
  24.0 4.7 %collective-permute-start.5 = (bf16[128,512]{1,0:T(8,128)(2,1)S(1)}, bf16[128,512]{1,0:T(8,128)(2,1)S(1)}, u32[]{:S(2)}, u32[]{:S(2)}) collective-permute-start(bf16[128,512]{1,0:T(8,128)(2,1)S(1)} %shard_map.41), channel_id=1, source_target_pairs={{0,128},{64,192},{128,0},{192,64},{1,129},{65,193},{129,1},{193,65... | collective-permute-start | bytes 393224 | tf_op jit(solution)/shard_map/ppermute | solution.py:27

commit v4 on v2

--- a/solution.py
+++ b/solution.py
@@ -1,3 +1,5 @@
+import functools
+
 import jax
 import jax.numpy as jnp
 from jax import lax
@@ -73,8 +75,9 @@
         acc[:, where] = jnp.dot(weighted[...], own[:, where], preferred_element_type=jnp.float32)
 
 
-def band_sum(halo, panels, acc, band, cells):
-    where = pl.ds(pl.multiple_of(band * cells, cells), cells)
+def band_sum(halo, panels, acc, band, cells, part=0, parts=1):
+    width = cells // parts
+    where = pl.ds(pl.multiple_of(band * cells + part * width, width), width)
     odd = lax.axis_index("lon") % 2
     total = acc[:, where]
     for (from_even, from_odd), h in zip(SHIFTS, halo):
@@ -83,9 +86,14 @@
     return total
 
 
-def far_body(ha, hb, hc, panels, acc, out):
+def far_body(part, ha, hb, hc, panels, acc, out):
     band = 3 - lax.axis_index("lat")
-    out[...] = band_sum((ha, hb, hc), panels, acc, band, ha.shape[1]).astype(out.dtype)
+    out[...] = band_sum((ha, hb, hc), panels, acc, band, ha.shape[1], part, 2).astype(out.dtype)
+
+
+def own_far_body(ha, hb, hc, panels, acc, mine):
+    band = lax.axis_index("lat")
+    mine[...] = band_sum((ha, hb, hc), panels, acc, (band + 2) % 4, ha.shape[1])
 
 
 def rest_body(ha, hb, hc, panels, acc, near, mine):
@@ -93,17 +101,20 @@
     partner = band + 1 - 2 * (band % 2)
     halo, cells = (ha, hb, hc), ha.shape[1]
     near[...] = band_sum(halo, panels, acc, partner, cells).astype(near.dtype)
-    mine[0] = band_sum(halo, panels, acc, 3 - partner, cells)
-    mine[1] = band_sum(halo, panels, acc, band, cells)
+    mine[...] = band_sum(halo, panels, acc, band, cells)
 
 
-def pack_body(mine, other, out):
-    out[...] = (mine[0] + other[...].astype(jnp.float32)).astype(out.dtype)
+def pack_body(part, mine, other, out):
+    width = out.shape[1]
+    out[...] = (mine[:, part * width : (part + 1) * width] + other[...].astype(jnp.float32)).astype(out.dtype)
 
 
-def final_body(mine, other, third, out):
-    total = mine[1] + other[...].astype(jnp.float32) + third[...].astype(jnp.float32)
-    out[...] = total.T
+def final_body(mine, other, third, fourth, out):
+    total = mine[...] + other[...].astype(jnp.float32)
+    width = third.shape[1]
+    for i, r in enumerate((third, fourth)):
+        here = slice(i * width, (i + 1) * width)
+        out[here, :] = (total[:, here] + r[...].astype(jnp.float32)).T
 
 
 def sweep(residual, noise_weights, kernel):
@@ -142,24 +153,32 @@
         8 * MB,
     )(weighted, in_hbm(kernel))
     flops = 6 * probes * cells * cells
-    far = call(far_body, shape((probes, cells), bf16), [VMEM] * 5, [], flops, 2 * MB, 8 * MB)(
+    half = shape((probes, cells // 2), bf16)
+    others = []
+    for i in range(2):
+        far = call(functools.partial(far_body, i), half, [VMEM] * 5, [], flops // 2, MB, 8 * MB)(
+            ha, hb, hc, kernel, acc
+        )
+        others.append(swapped(far, 1))
+    own_far = call(own_far_body, shape((probes, cells), f32), [VMEM] * 5, [], flops, 2 * MB, 8 * MB)(
         ha, hb, hc, kernel, acc
     )
-    other_far = swapped(far, 1)
+    thirds = []
+    for i in range(2):
+        packed = call(functools.partial(pack_body, i), half, [VMEM] * 2, [], 0, MB // 2, 4 * MB)(own_far, others[i])
+        thirds.append(swapped(packed, 2))
     near, mine = call(
         rest_body,
-        (shape((probes, cells), bf16), shape((2, probes, cells), f32)),
+        (shape((probes, cells), bf16), shape((probes, cells), f32)),
         [VMEM] * 5,
         [],
-        3 * flops,
-        6 * MB,
+        2 * flops,
+        4 * MB,
         8 * MB,
     )(ha, hb, hc, kernel, acc)
-    packed = call(pack_body, shape((probes, cells), bf16), [VMEM] * 2, [], 0, MB, 4 * MB)(mine, other_far)
-    third = swapped(packed, 2)
     other_near = swapped(near, 1)
-    total = call(final_body, shape((cells, probes), f32), [VMEM] * 3, [], 0, MB, 4 * MB)(
-        mine, other_near, third
+    total = call(final_body, shape((cells, probes), f32), [VMEM] * 4, [], 0, MB, 4 * MB)(
+        mine, other_near, *thirds
     )
     return total.reshape(1, rows, columns, probes)
 

time: 29.7 us -> 28.2 us (0.949)
  waiting for transfers between devices: 14.5 us -> 11.4 us
  starting transfers between devices: 9.83 us -> 11 us
  Pallas kernels: 5.21 us -> 5.59 us
    ppermute x3 -> x5, starting transfers between devices: 1.92 us -> 5.01 us  [swapped(): return lax.ppermute(value, 'lat', [(i, i ^ mask) for i in range(length)])]
    ppermute x3, waiting for transfers between devices: 10.2 us -> 7.94 us  [eastward(): return lax.ppermute(value, 'lon', pairs)]
    ppermute x3, starting transfers between devices: 7.91 us -> 6 us  [eastward(): return lax.ppermute(value, 'lon', pairs)]
    ppermute x3 -> x5, waiting for transfers between devices: 4.32 us -> 3.45 us  [swapped(): return lax.ppermute(value, 'lat', [(i, i ^ mask) for i in range(length)])]
    pallas_call x4 -> x7, Pallas kernels: 2.05 us -> 2.43 us  [the longest x1 0.84 us: sweep(): call(final_body, shape((cells, probes), f32), [VMEM] * 4, [], 0, MB, 4 * MB)]
  transfers between devices with their start and end apart: 6 -> 8, of which waited for: 6 -> 4; matrix products, arithmetic and copies ran while one was open for 0% -> 0% of each run, Pallas kernels for 10% -> 12%
where the time goes in v4:
time: 28.2 us; the launch traced here: 28.1 us
  waiting for transfers between devices  11.4 us (40%)
  starting transfers between devices  11 us (39%)
  Pallas kernels  5.59 us (20%)
    ppermute x3, waiting for transfers between devices, eastward(): return lax.ppermute(value, 'lon', pairs)  7.94 us
    ppermute x3, starting transfers between devices, eastward(): return lax.ppermute(value, 'lon', pairs)  6 us
    ppermute x5, starting transfers between devices, swapped(): return lax.ppermute(value, 'lat', [(i, i ^ mask) for i in range(length)])  5.01 us
    ppermute x5, waiting for transfers between devices, swapped(): return lax.ppermute(value, 'lat', [(i, i ^ mask) for i in range(length)])  3.45 us
    pallas_call x1, Pallas kernels, sweep(): call(first_body, shape((probes, every), f32), [VMEM, HBM], [pltpu.VMEM((c...  2 us
    pallas_call x1, Pallas kernels, sweep(): call(weigh_body, pltpu.VMEM((probes, cells), bf16), [HBM] * 2, [pltpu.VME...  1.16 us
    pallas_call x1, Pallas kernels, sweep(): call(final_body, shape((cells, probes), f32), [VMEM] * 4, [], 0, MB, 4 * MB)  0.84 us
    pallas_call x1, Pallas kernels, sweep(): call(rest_body, (shape((probes, cells), bf16), shape((probes, cells), f32...  0.59 us
  transfers between devices with their start and end apart: 8, of which 4 were waited for; matrix products, arithmetic and copies ran while one was open for 0% of the time, Pallas kernels for 12%

profile of v4, /device:TPU:1, one launch (start us, length us, event | category | flops | bytes accessed | tf_op | source)
XLA Modules:
  0.0 28.1 jit_solution(8667046910938831933)
XLA Ops:
  0.0 1.2 %shard_map.37.weighted = bf16[128,512]{1,0:T(8,128)(2,1)S(1)} custom-call(bf16[32,16,128]{2,1,0:T(8,128)(2,1)} %residual.1, f32[16,32]{1,0:T(8,128)} %bitcast.2), custom_call_target="tpu_custom_call" | custom-call | bytes 262144 | tf_op jit(solution)/shard_map/pallas_call | solution.py:128
  1.2 0.0 copy-start
  1.2 4.7 %collective-permute-start = (bf16[128,512]{1,0:T(8,128)(2,1)S(1)}, bf16[128,512]{1,0:T(8,128)(2,1)S(1)}, u32[]{:S(2)}, u32[]{:S(2)}) collective-permute-start(bf16[128,512]{1,0:T(8,128)(2,1)S(1)} %shard_map.37.weighted), channel_id=1, source_target_pairs={{0,3},{1,2},{2,5},{3,4},{4,7},{5,6},{6,9},{7,8},{8,11},{9,10},{10,... | collective-permute-start | bytes 393224 | tf_op jit(solution)/shard_map/ppermute | solution.py:24
  5.9 0.1 collective-permute-start.1
  6.0 1.2 %collective-permute-start.2 = (bf16[128,512]{1,0:T(8,128)(2,1)S(1)}, bf16[128,512]{1,0:T(8,128)(2,1)S(1)}, u32[]{:S(2)}, u32[]{:S(2)}) collective-permute-start(bf16[128,512]{1,0:T(8,128)(2,1)S(1)} %shard_map.37.weighted), channel_id=1, source_target_pairs={{0,2},{1,3},{2,4},{3,5},{4,6},{5,7},{6,8},{7,9},{8,10},{9,11},{10,... | collective-permute-start | bytes 393224 | tf_op jit(solution)/shard_map/ppermute | solution.py:24
  7.2 2.0 %shard_map.38.acc = f32[128,2048]{1,0:T(8,128)S(1)} custom-call(bf16[128,512]{1,0:T(8,128)(2,1)S(1)} %shard_map.37.weighted, bf16[4,1,512,2048]{3,2,1,0:T(8,128)(2,1)} %panels.9), custom_call_target="tpu_custom_call" | custom-call | flops 268435456 | bytes 3145728 | tf_op jit(solution)/shard_map/pallas_call | solution.py:146
  9.2 7.2 %collective-permute-done.ha = bf16[128,512]{1,0:T(8,128)(2,1)S(1)} collective-permute-done((bf16[128,512]{1,0:T(8,128)(2,1)S(1)}, bf16[128,512]{1,0:T(8,128)(2,1)S(1)}, u32[]{:S(2)}, u32[]{:S(2)}) %collective-permute-start) | collective-permute-done | bytes 131104 | tf_op jit(solution)/shard_map/ppermute | solution.py:24
  16.4 0.7 %collective-permute-done.1.hb = bf16[128,512]{1,0:T(8,128)(2,1)S(1)} collective-permute-done((bf16[128,512]{1,0:T(8,128)(2,1)S(1)}, bf16[128,512]{1,0:T(8,128)(2,1)S(1)}, u32[]{:S(2)}, u32[]{:S(2)}) %collective-permute-start.1) | collective-permute-done | bytes 131104 | tf_op jit(solution)/shard_map/ppermute | solution.py:24
  17.1 0.0 collective-permute-done.2.hc
  17.1 0.0 copy-done
  17.1 0.3 %shard_map.43 = bf16[128,256]{1,0:T(8,128)(2,1)S(1)} custom-call(bf16[128,512]{1,0:T(8,128)(2,1)S(1)} %collective-permute-done.ha, bf16[128,512]{1,0:T(8,128)(2,1)S(1)} %collective-permute-done.1.hb, bf16[128,512]{1,0:T(8,128)(2,1)S(1)} %collective-permute-done.2.hc, bf16[4,1,512,2048]{3,2,1,0:T(8,128)(2,1)S(1)} %copy-done, f32[128,2048]{1,0:T(8,128)S(1)} %shard_map.38.acc), custom_call_target="tpu_custom_call" | custom-call | flops 100663296 | bytes 1048576 | tf_op jit(solution)/shard_map/pallas_call | solution.py:159
  17.4 2.7 %collective-permute-start.6 = (bf16[128,256]{1,0:T(8,128)(2,1)S(1)}, bf16[128,256]{1,0:T(8,128)(2,1)S(1)}, u32[]{:S(2)}, u32[]{:S(2)}) collective-permute-start(bf16[128,256]{1,0:T(8,128)(2,1)S(1)} %shard_map.43), channel_id=1, source_target_pairs={{0,64},{64,0},{128,192},{192,128},{1,65},{65,1},{129,193},{193,129... | collective-permute-start | bytes 196616 | tf_op jit(solution)/shard_map/ppermute | solution.py:29
  20.1 0.3 %shard_map.41 = bf16[128,256]{1,0:T(8,128)(2,1)S(1)} custom-call(bf16[128,512]{1,0:T(8,128)(2,1)S(1)} %collective-permute-done.ha, bf16[128,512]{1,0:T(8,128)(2,1)S(1)} %collective-permute-done.1.hb, bf16[128,512]{1,0:T(8,128)(2,1)S(1)} %collective-permute-done.2.hc, bf16[4,1,512,2048]{3,2,1,0:T(8,128)(2,1)S(1)} %copy-done, f32[128,2048]{1,0:T(8,128)S(1)} %shard_map.38.acc), custom_call_target="tpu_custom_call" | custom-call | flops 100663296 | bytes 1048576 | tf_op jit(solution)/shard_map/pallas_call | solution.py:159
  20.4 0.1 collective-permute-start.4
  20.5 0.6 %shard_map.39 = (bf16[128,512]{1,0:T(8,128)(2,1)S(1)}, f32[128,512]{1,0:T(8,128)S(1)}) custom-call(bf16[128,512]{1,0:T(8,128)(2,1)S(1)} %collective-permute-done.ha, bf16[128,512]{1,0:T(8,128)(2,1)S(1)} %collective-permute-done.1.hb, bf16[128,512]{1,0:T(8,128)(2,1)S(1)} %collective-permute-done.2.hc, bf16[4,1,512,2048]{3,2,1,0:T(8,128)(2,1)S(1)} %copy-done, ...), custom_call_target="tpu_custom_call" | custom-call | flops 402653184 | bytes 4194304 | tf_op jit(solution)/shard_map/pallas_call | solution.py:170
  21.1 0.6 %collective-permute-start.3 = (bf16[128,512]{1,0:T(8,128)(2,1)S(1)}, bf16[128,512]{1,0:T(8,128)(2,1)S(1)}, u32[]{:S(2)}, u32[]{:S(2)}) collective-permute-start(bf16[128,512]{1,0:T(8,128)(2,1)S(1)} %get-tuple-element.8), channel_id=1, source_target_pairs={{0,64},{64,0},{128,192},{192,128},{1,65},{65,1},{129,193},{193,129... | collective-permute-start | bytes 393224 | tf_op jit(solution)/shard_map/ppermute | solution.py:29
  21.7 0.4 %shard_map.40.mine = f32[128,512]{1,0:T(8,128)S(1)} custom-call(bf16[128,512]{1,0:T(8,128)(2,1)S(1)} %collective-permute-done.ha, bf16[128,512]{1,0:T(8,128)(2,1)S(1)} %collective-permute-done.1.hb, bf16[128,512]{1,0:T(8,128)(2,1)S(1)} %collective-permute-done.2.hc, bf16[4,1,512,2048]{3,2,1,0:T(8,128)(2,1)S(1)} %copy-done, f32[128,2048]{1,0:T(8,128)S(1)} %shard_map.38.acc), custom_call_target="tpu_custom_call" | custom-call | flops 201326592 | bytes 2097152 | tf_op jit(solution)/shard_map/pallas_call | solution.py:163
  22.1 0.0 collective-permute-done.6.other
  22.1 0.7 %collective-permute-start.7 = (bf16[128,256]{1,0:T(8,128)(2,1)S(1)}, bf16[128,256]{1,0:T(8,128)(2,1)S(1)}, u32[]{:S(2)}, u32[]{:S(2)}) collective-permute-start(bf16[128,256]{1,0:T(8,128)(2,1)S(1)} %shard_map.44), channel_id=1, source_target_pairs={{0,128},{64,192},{128,0},{192,64},{1,129},{65,193},{129,1},{193,65... | collective-permute-start | bytes 196616 | tf_op jit(solution)/shard_map/ppermute | solution.py:29
  22.8 0.0 collective-permute-done.4.other
  22.8 1.0 %collective-permute-start.5 = (bf16[128,256]{1,0:T(8,128)(2,1)S(1)}, bf16[128,256]{1,0:T(8,128)(2,1)S(1)}, u32[]{:S(2)}, u32[]{:S(2)}) collective-permute-start(bf16[128,256]{1,0:T(8,128)(2,1)S(1)} %shard_map.42), channel_id=1, source_target_pairs={{0,128},{64,192},{128,0},{192,64},{1,129},{65,193},{129,1},{193,65... | collective-permute-start | bytes 196616 | tf_op jit(solution)/shard_map/ppermute | solution.py:29
  23.8 2.0 %collective-permute-done.7.fourth = bf16[128,256]{1,0:T(8,128)(2,1)S(1)} collective-permute-done((bf16[128,256]{1,0:T(8,128)(2,1)S(1)}, bf16[128,256]{1,0:T(8,128)(2,1)S(1)}, u32[]{:S(2)}, u32[]{:S(2)}) %collective-permute-start.7) | collective-permute-done | bytes 65568 | tf_op jit(solution)/shard_map/ppermute | solution.py:29
  25.8 1.4 %collective-permute-done.5.third = bf16[128,256]{1,0:T(8,128)(2,1)S(1)} collective-permute-done((bf16[128,256]{1,0:T(8,128)(2,1)S(1)}, bf16[128,256]{1,0:T(8,128)(2,1)S(1)}, u32[]{:S(2)}, u32[]{:S(2)}) %collective-permute-start.5) | collective-permute-done | bytes 65568 | tf_op jit(solution)/shard_map/ppermute | solution.py:29
  27.2 0.0 collective-permute-done.3.other
  27.2 0.8 %shard_map.45 = f32[512,128]{1,0:T(8,128)} custom-call(f32[128,512]{1,0:T(8,128)S(1)} %get-tuple-element.7.mine, bf16[128,512]{1,0:T(8,128)(2,1)S(1)} %collective-permute-done.3.other, bf16[128,256]{1,0:T(8,128)(2,1)S(1)} %collective-permute-done.5.third, bf16[128,256]{1,0:T(8,128)(2,1)S(1)} %collective-permute-done.7.fourth), custom_call_target="tpu_custom_call" | custom-call | bytes 1048576 | tf_op jit(solution)/shard_map/pallas_call | solution.py:180
  (2 shorter events, 0.0 us)
Async XLA Ops:
  1.2 16.0 %copy-start = (bf16[4,1,512,2048]{3,2,1,0:T(8,128)(2,1)S(1)}, bf16[4,1,512,2048]{3,2,1,0:T(8,128)(2,1)}, u32[]{:S(2)}) copy-start(bf16[4,1,512,2048]{3,2,1,0:T(8,128)(2,1)} %panels.9) | copy-start | bytes 25165828
  1.2 15.2 %collective-permute-start = (bf16[128,512]{1,0:T(8,128)(2,1)S(1)}, bf16[128,512]{1,0:T(8,128)(2,1)S(1)}, u32[]{:S(2)}, u32[]{:S(2)}) collective-permute-start(bf16[128,512]{1,0:T(8,128)(2,1)S(1)} %shard_map.37.weighted), channel_id=1, source_target_pairs={{0,3},{1,2},{2,5},{3,4},{4,7},{5,6},{6,9},{7,8},{8,11},{9,10},{10,... | collective-permute-start | bytes 393224 | tf_op jit(solution)/shard_map/ppermute | solution.py:24
  5.9 11.2 %collective-permute-start.1 = (bf16[128,512]{1,0:T(8,128)(2,1)S(1)}, bf16[128,512]{1,0:T(8,128)(2,1)S(1)}, u32[]{:S(2)}, u32[]{:S(2)}) collective-permute-start(bf16[128,512]{1,0:T(8,128)(2,1)S(1)} %shard_map.37.weighted), channel_id=1, source_target_pairs={{0,1},{1,4},{2,3},{3,6},{4,5},{5,8},{6,7},{7,10},{8,9},{9,12},{10,... | collective-permute-start | bytes 393224 | tf_op jit(solution)/shard_map/ppermute | solution.py:24
  6.0 11.2 %collective-permute-start.2 = (bf16[128,512]{1,0:T(8,128)(2,1)S(1)}, bf16[128,512]{1,0:T(8,128)(2,1)S(1)}, u32[]{:S(2)}, u32[]{:S(2)}) collective-permute-start(bf16[128,512]{1,0:T(8,128)(2,1)S(1)} %shard_map.37.weighted), channel_id=1, source_target_pairs={{0,2},{1,3},{2,4},{3,5},{4,6},{5,7},{6,8},{7,9},{8,10},{9,11},{10,... | collective-permute-start | bytes 393224 | tf_op jit(solution)/shard_map/ppermute | solution.py:24
  17.4 4.7 %collective-permute-start.6 = (bf16[128,256]{1,0:T(8,128)(2,1)S(1)}, bf16[128,256]{1,0:T(8,128)(2,1)S(1)}, u32[]{:S(2)}, u32[]{:S(2)}) collective-permute-start(bf16[128,256]{1,0:T(8,128)(2,1)S(1)} %shard_map.43), channel_id=1, source_target_pairs={{0,64},{64,0},{128,192},{192,128},{1,65},{65,1},{129,193},{193,129... | collective-permute-start | bytes 196616 | tf_op jit(solution)/shard_map/ppermute | solution.py:29
  20.4 2.4 %collective-permute-start.4 = (bf16[128,256]{1,0:T(8,128)(2,1)S(1)}, bf16[128,256]{1,0:T(8,128)(2,1)S(1)}, u32[]{:S(2)}, u32[]{:S(2)}) collective-permute-start(bf16[128,256]{1,0:T(8,128)(2,1)S(1)} %shard_map.41), channel_id=1, source_target_pairs={{0,64},{64,0},{128,192},{192,128},{1,65},{65,1},{129,193},{193,129... | collective-permute-start | bytes 196616 | tf_op jit(solution)/shard_map/ppermute | solution.py:29
  21.1 6.1 %collective-permute-start.3 = (bf16[128,512]{1,0:T(8,128)(2,1)S(1)}, bf16[128,512]{1,0:T(8,128)(2,1)S(1)}, u32[]{:S(2)}, u32[]{:S(2)}) collective-permute-start(bf16[128,512]{1,0:T(8,128)(2,1)S(1)} %get-tuple-element.8), channel_id=1, source_target_pairs={{0,64},{64,0},{128,192},{192,128},{1,65},{65,1},{129,193},{193,129... | collective-permute-start | bytes 393224 | tf_op jit(solution)/shard_map/ppermute | solution.py:29
  22.1 3.7 %collective-permute-start.7 = (bf16[128,256]{1,0:T(8,128)(2,1)S(1)}, bf16[128,256]{1,0:T(8,128)(2,1)S(1)}, u32[]{:S(2)}, u32[]{:S(2)}) collective-permute-start(bf16[128,256]{1,0:T(8,128)(2,1)S(1)} %shard_map.44), channel_id=1, source_target_pairs={{0,128},{64,192},{128,0},{192,64},{1,129},{65,193},{129,1},{193,65... | collective-permute-start | bytes 196616 | tf_op jit(solution)/shard_map/ppermute | solution.py:29
  22.8 4.4 %collective-permute-start.5 = (bf16[128,256]{1,0:T(8,128)(2,1)S(1)}, bf16[128,256]{1,0:T(8,128)(2,1)S(1)}, u32[]{:S(2)}, u32[]{:S(2)}) collective-permute-start(bf16[128,256]{1,0:T(8,128)(2,1)S(1)} %shard_map.42), channel_id=1, source_target_pairs={{0,128},{64,192},{128,0},{192,64},{1,129},{65,193},{129,1},{193,65... | collective-permute-start | bytes 196616 | tf_op jit(solution)/shard_map/ppermute | solution.py:29

commit v5 on v4

--- a/solution.py
+++ b/solution.py
@@ -109,12 +109,18 @@
     out[...] = (mine[:, part * width : (part + 1) * width] + other[...].astype(jnp.float32)).astype(out.dtype)
 
 
-def final_body(mine, other, third, fourth, out):
-    total = mine[...] + other[...].astype(jnp.float32)
+def final_body(mine, other, third, fourth, out, rows, sems):
     width = third.shape[1]
+    copies = []
     for i, r in enumerate((third, fourth)):
         here = slice(i * width, (i + 1) * width)
-        out[here, :] = (total[:, here] + r[...].astype(jnp.float32)).T
+        total = mine[:, here] + other[:, here].astype(jnp.float32) + r[...].astype(jnp.float32)
+        rows[here, :] = total.T
+        part = pl.ds(i * width, width)
+        copies.append(pltpu.make_async_copy(rows.at[part], out.at[part], sems.at[i]))
+        copies[i].start()
+    for copy in copies:
+        copy.wait()
 
 
 def sweep(residual, noise_weights, kernel):
@@ -177,9 +183,14 @@
         8 * MB,
     )(ha, hb, hc, kernel, acc)
     other_near = swapped(near, 1)
-    total = call(final_body, shape((cells, probes), f32), [VMEM] * 4, [], 0, MB, 4 * MB)(
-        mine, other_near, *thirds
-    )
+    total = pl.pallas_call(
+        final_body,
+        out_shape=shape((cells, probes), f32),
+        in_specs=[VMEM] * 4,
+        out_specs=HBM,
+        scratch_shapes=[pltpu.VMEM((cells, probes), f32), pltpu.SemaphoreType.DMA((2,))],
+        compiler_params=pltpu.CompilerParams(vmem_limit_bytes=4 * MB),
+    )(mine, other_near, *thirds)
     return total.reshape(1, rows, columns, probes)
 
 

time: 28.2 us -> 28.2 us (level)
  no operation moved by 1% of the time
where the time goes in v5:
time: 28.2 us; the launch traced here: 28.1 us
  waiting for transfers between devices  11.4 us (40%)
  starting transfers between devices  11 us (39%)
  Pallas kernels  5.57 us (20%)
    ppermute x3, waiting for transfers between devices, eastward(): return lax.ppermute(value, 'lon', pairs)  7.94 us
    ppermute x3, starting transfers between devices, eastward(): return lax.ppermute(value, 'lon', pairs)  6 us
    ppermute x5, starting transfers between devices, swapped(): return lax.ppermute(value, 'lat', [(i, i ^ mask) for i in range(length)])  5.01 us
    ppermute x5, waiting for transfers between devices, swapped(): return lax.ppermute(value, 'lat', [(i, i ^ mask) for i in range(length)])  3.45 us
    pallas_call x1, Pallas kernels, sweep(): call(first_body, shape((probes, every), f32), [VMEM, HBM], [pltpu.VMEM((c...  2 us
    pallas_call x1, Pallas kernels, sweep(): call(weigh_body, pltpu.VMEM((probes, cells), bf16), [HBM] * 2, [pltpu.VME...  1.16 us
    pallas_call x1, Pallas kernels, sweep(): pl.pallas_call(final_body, out_shape=shape((cells, probes), f32), in_spec...  0.82 us
    pallas_call x1, Pallas kernels, sweep(): call(rest_body, (shape((probes, cells), bf16), shape((probes, cells), f32...  0.59 us
  transfers between devices with their start and end apart: 8, of which 4 were waited for; matrix products, arithmetic and copies ran while one was open for 0% of the time, Pallas kernels for 12%

profile of v5, /device:TPU:1, one launch (start us, length us, event | category | flops | bytes accessed | tf_op | source)
XLA Modules:
  0.0 28.1 jit_solution(14953936095934576210)
XLA Ops:
  0.0 1.2 %shard_map.37.weighted = bf16[128,512]{1,0:T(8,128)(2,1)S(1)} custom-call(bf16[32,16,128]{2,1,0:T(8,128)(2,1)} %residual.1, f32[16,32]{1,0:T(8,128)} %bitcast.2), custom_call_target="tpu_custom_call" | custom-call | bytes 262144 | tf_op jit(solution)/shard_map/pallas_call | solution.py:134
  1.2 0.0 copy-start
  1.2 4.7 %collective-permute-start = (bf16[128,512]{1,0:T(8,128)(2,1)S(1)}, bf16[128,512]{1,0:T(8,128)(2,1)S(1)}, u32[]{:S(2)}, u32[]{:S(2)}) collective-permute-start(bf16[128,512]{1,0:T(8,128)(2,1)S(1)} %shard_map.37.weighted), channel_id=1, source_target_pairs={{0,3},{1,2},{2,5},{3,4},{4,7},{5,6},{6,9},{7,8},{8,11},{9,10},{10,... | collective-permute-start | bytes 393224 | tf_op jit(solution)/shard_map/ppermute | solution.py:24
  5.9 0.1 collective-permute-start.1
  6.0 1.2 %collective-permute-start.2 = (bf16[128,512]{1,0:T(8,128)(2,1)S(1)}, bf16[128,512]{1,0:T(8,128)(2,1)S(1)}, u32[]{:S(2)}, u32[]{:S(2)}) collective-permute-start(bf16[128,512]{1,0:T(8,128)(2,1)S(1)} %shard_map.37.weighted), channel_id=1, source_target_pairs={{0,2},{1,3},{2,4},{3,5},{4,6},{5,7},{6,8},{7,9},{8,10},{9,11},{10,... | collective-permute-start | bytes 393224 | tf_op jit(solution)/shard_map/ppermute | solution.py:24
  7.2 2.0 %shard_map.38.acc = f32[128,2048]{1,0:T(8,128)S(1)} custom-call(bf16[128,512]{1,0:T(8,128)(2,1)S(1)} %shard_map.37.weighted, bf16[4,1,512,2048]{3,2,1,0:T(8,128)(2,1)} %panels.9), custom_call_target="tpu_custom_call" | custom-call | flops 268435456 | bytes 3145728 | tf_op jit(solution)/shard_map/pallas_call | solution.py:152
  9.2 7.2 %collective-permute-done.ha = bf16[128,512]{1,0:T(8,128)(2,1)S(1)} collective-permute-done((bf16[128,512]{1,0:T(8,128)(2,1)S(1)}, bf16[128,512]{1,0:T(8,128)(2,1)S(1)}, u32[]{:S(2)}, u32[]{:S(2)}) %collective-permute-start) | collective-permute-done | bytes 131104 | tf_op jit(solution)/shard_map/ppermute | solution.py:24
  16.4 0.7 %collective-permute-done.1.hb = bf16[128,512]{1,0:T(8,128)(2,1)S(1)} collective-permute-done((bf16[128,512]{1,0:T(8,128)(2,1)S(1)}, bf16[128,512]{1,0:T(8,128)(2,1)S(1)}, u32[]{:S(2)}, u32[]{:S(2)}) %collective-permute-start.1) | collective-permute-done | bytes 131104 | tf_op jit(solution)/shard_map/ppermute | solution.py:24
  17.1 0.0 collective-permute-done.2.hc
  17.1 0.0 copy-done
  17.1 0.3 %shard_map.43 = bf16[128,256]{1,0:T(8,128)(2,1)S(1)} custom-call(bf16[128,512]{1,0:T(8,128)(2,1)S(1)} %collective-permute-done.ha, bf16[128,512]{1,0:T(8,128)(2,1)S(1)} %collective-permute-done.1.hb, bf16[128,512]{1,0:T(8,128)(2,1)S(1)} %collective-permute-done.2.hc, bf16[4,1,512,2048]{3,2,1,0:T(8,128)(2,1)S(1)} %copy-done, f32[128,2048]{1,0:T(8,128)S(1)} %shard_map.38.acc), custom_call_target="tpu_custom_call" | custom-call | flops 100663296 | bytes 1048576 | tf_op jit(solution)/shard_map/pallas_call | solution.py:165
  17.4 2.7 %collective-permute-start.6 = (bf16[128,256]{1,0:T(8,128)(2,1)S(1)}, bf16[128,256]{1,0:T(8,128)(2,1)S(1)}, u32[]{:S(2)}, u32[]{:S(2)}) collective-permute-start(bf16[128,256]{1,0:T(8,128)(2,1)S(1)} %shard_map.43), channel_id=1, source_target_pairs={{0,64},{64,0},{128,192},{192,128},{1,65},{65,1},{129,193},{193,129... | collective-permute-start | bytes 196616 | tf_op jit(solution)/shard_map/ppermute | solution.py:29
  20.1 0.3 %shard_map.41 = bf16[128,256]{1,0:T(8,128)(2,1)S(1)} custom-call(bf16[128,512]{1,0:T(8,128)(2,1)S(1)} %collective-permute-done.ha, bf16[128,512]{1,0:T(8,128)(2,1)S(1)} %collective-permute-done.1.hb, bf16[128,512]{1,0:T(8,128)(2,1)S(1)} %collective-permute-done.2.hc, bf16[4,1,512,2048]{3,2,1,0:T(8,128)(2,1)S(1)} %copy-done, f32[128,2048]{1,0:T(8,128)S(1)} %shard_map.38.acc), custom_call_target="tpu_custom_call" | custom-call | flops 100663296 | bytes 1048576 | tf_op jit(solution)/shard_map/pallas_call | solution.py:165
  20.4 0.1 collective-permute-start.4
  20.5 0.6 %shard_map.39 = (bf16[128,512]{1,0:T(8,128)(2,1)S(1)}, f32[128,512]{1,0:T(8,128)S(1)}) custom-call(bf16[128,512]{1,0:T(8,128)(2,1)S(1)} %collective-permute-done.ha, bf16[128,512]{1,0:T(8,128)(2,1)S(1)} %collective-permute-done.1.hb, bf16[128,512]{1,0:T(8,128)(2,1)S(1)} %collective-permute-done.2.hc, bf16[4,1,512,2048]{3,2,1,0:T(8,128)(2,1)S(1)} %copy-done, ...), custom_call_target="tpu_custom_call" | custom-call | flops 402653184 | bytes 4194304 | tf_op jit(solution)/shard_map/pallas_call | solution.py:176
  21.1 0.6 %collective-permute-start.3 = (bf16[128,512]{1,0:T(8,128)(2,1)S(1)}, bf16[128,512]{1,0:T(8,128)(2,1)S(1)}, u32[]{:S(2)}, u32[]{:S(2)}) collective-permute-start(bf16[128,512]{1,0:T(8,128)(2,1)S(1)} %get-tuple-element.8), channel_id=1, source_target_pairs={{0,64},{64,0},{128,192},{192,128},{1,65},{65,1},{129,193},{193,129... | collective-permute-start | bytes 393224 | tf_op jit(solution)/shard_map/ppermute | solution.py:29
  21.7 0.4 %shard_map.40.mine = f32[128,512]{1,0:T(8,128)S(1)} custom-call(bf16[128,512]{1,0:T(8,128)(2,1)S(1)} %collective-permute-done.ha, bf16[128,512]{1,0:T(8,128)(2,1)S(1)} %collective-permute-done.1.hb, bf16[128,512]{1,0:T(8,128)(2,1)S(1)} %collective-permute-done.2.hc, bf16[4,1,512,2048]{3,2,1,0:T(8,128)(2,1)S(1)} %copy-done, f32[128,2048]{1,0:T(8,128)S(1)} %shard_map.38.acc), custom_call_target="tpu_custom_call" | custom-call | flops 201326592 | bytes 2097152 | tf_op jit(solution)/shard_map/pallas_call | solution.py:169
  22.1 0.0 collective-permute-done.6.other
  22.1 0.7 %collective-permute-start.7 = (bf16[128,256]{1,0:T(8,128)(2,1)S(1)}, bf16[128,256]{1,0:T(8,128)(2,1)S(1)}, u32[]{:S(2)}, u32[]{:S(2)}) collective-permute-start(bf16[128,256]{1,0:T(8,128)(2,1)S(1)} %shard_map.44), channel_id=1, source_target_pairs={{0,128},{64,192},{128,0},{192,64},{1,129},{65,193},{129,1},{193,65... | collective-permute-start | bytes 196616 | tf_op jit(solution)/shard_map/ppermute | solution.py:29
  22.8 0.0 collective-permute-done.4.other
  22.8 1.0 %collective-permute-start.5 = (bf16[128,256]{1,0:T(8,128)(2,1)S(1)}, bf16[128,256]{1,0:T(8,128)(2,1)S(1)}, u32[]{:S(2)}, u32[]{:S(2)}) collective-permute-start(bf16[128,256]{1,0:T(8,128)(2,1)S(1)} %shard_map.42), channel_id=1, source_target_pairs={{0,128},{64,192},{128,0},{192,64},{1,129},{65,193},{129,1},{193,65... | collective-permute-start | bytes 196616 | tf_op jit(solution)/shard_map/ppermute | solution.py:29
  23.8 2.0 %collective-permute-done.7.fourth = bf16[128,256]{1,0:T(8,128)(2,1)S(1)} collective-permute-done((bf16[128,256]{1,0:T(8,128)(2,1)S(1)}, bf16[128,256]{1,0:T(8,128)(2,1)S(1)}, u32[]{:S(2)}, u32[]{:S(2)}) %collective-permute-start.7) | collective-permute-done | bytes 65568 | tf_op jit(solution)/shard_map/ppermute | solution.py:29
  25.8 1.4 %collective-permute-done.5.third = bf16[128,256]{1,0:T(8,128)(2,1)S(1)} collective-permute-done((bf16[128,256]{1,0:T(8,128)(2,1)S(1)}, bf16[128,256]{1,0:T(8,128)(2,1)S(1)}, u32[]{:S(2)}, u32[]{:S(2)}) %collective-permute-start.5) | collective-permute-done | bytes 65568 | tf_op jit(solution)/shard_map/ppermute | solution.py:29
  27.2 0.0 collective-permute-done.3.other
  27.2 0.8 %shard_map.45 = f32[512,128]{1,0:T(8,128)} custom-call(f32[128,512]{1,0:T(8,128)S(1)} %get-tuple-element.7.mine, bf16[128,512]{1,0:T(8,128)(2,1)S(1)} %collective-permute-done.3.other, bf16[128,256]{1,0:T(8,128)(2,1)S(1)} %collective-permute-done.5.third, bf16[128,256]{1,0:T(8,128)(2,1)S(1)} %collective-permute-done.7.fourth), custom_call_target="tpu_custom_call" | custom-call | tf_op jit(solution)/shard_map/pallas_call | solution.py:186
  (2 shorter events, 0.0 us)
Async XLA Ops:
  1.2 16.0 %copy-start = (bf16[4,1,512,2048]{3,2,1,0:T(8,128)(2,1)S(1)}, bf16[4,1,512,2048]{3,2,1,0:T(8,128)(2,1)}, u32[]{:S(2)}) copy-start(bf16[4,1,512,2048]{3,2,1,0:T(8,128)(2,1)} %panels.9) | copy-start | bytes 25165828
  1.2 15.2 %collective-permute-start = (bf16[128,512]{1,0:T(8,128)(2,1)S(1)}, bf16[128,512]{1,0:T(8,128)(2,1)S(1)}, u32[]{:S(2)}, u32[]{:S(2)}) collective-permute-start(bf16[128,512]{1,0:T(8,128)(2,1)S(1)} %shard_map.37.weighted), channel_id=1, source_target_pairs={{0,3},{1,2},{2,5},{3,4},{4,7},{5,6},{6,9},{7,8},{8,11},{9,10},{10,... | collective-permute-start | bytes 393224 | tf_op jit(solution)/shard_map/ppermute | solution.py:24
  5.9 11.2 %collective-permute-start.1 = (bf16[128,512]{1,0:T(8,128)(2,1)S(1)}, bf16[128,512]{1,0:T(8,128)(2,1)S(1)}, u32[]{:S(2)}, u32[]{:S(2)}) collective-permute-start(bf16[128,512]{1,0:T(8,128)(2,1)S(1)} %shard_map.37.weighted), channel_id=1, source_target_pairs={{0,1},{1,4},{2,3},{3,6},{4,5},{5,8},{6,7},{7,10},{8,9},{9,12},{10,... | collective-permute-start | bytes 393224 | tf_op jit(solution)/shard_map/ppermute | solution.py:24
  6.0 11.2 %collective-permute-start.2 = (bf16[128,512]{1,0:T(8,128)(2,1)S(1)}, bf16[128,512]{1,0:T(8,128)(2,1)S(1)}, u32[]{:S(2)}, u32[]{:S(2)}) collective-permute-start(bf16[128,512]{1,0:T(8,128)(2,1)S(1)} %shard_map.37.weighted), channel_id=1, source_target_pairs={{0,2},{1,3},{2,4},{3,5},{4,6},{5,7},{6,8},{7,9},{8,10},{9,11},{10,... | collective-permute-start | bytes 393224 | tf_op jit(solution)/shard_map/ppermute | solution.py:24
  17.4 4.7 %collective-permute-start.6 = (bf16[128,256]{1,0:T(8,128)(2,1)S(1)}, bf16[128,256]{1,0:T(8,128)(2,1)S(1)}, u32[]{:S(2)}, u32[]{:S(2)}) collective-permute-start(bf16[128,256]{1,0:T(8,128)(2,1)S(1)} %shard_map.43), channel_id=1, source_target_pairs={{0,64},{64,0},{128,192},{192,128},{1,65},{65,1},{129,193},{193,129... | collective-permute-start | bytes 196616 | tf_op jit(solution)/shard_map/ppermute | solution.py:29
  20.4 2.4 %collective-permute-start.4 = (bf16[128,256]{1,0:T(8,128)(2,1)S(1)}, bf16[128,256]{1,0:T(8,128)(2,1)S(1)}, u32[]{:S(2)}, u32[]{:S(2)}) collective-permute-start(bf16[128,256]{1,0:T(8,128)(2,1)S(1)} %shard_map.41), channel_id=1, source_target_pairs={{0,64},{64,0},{128,192},{192,128},{1,65},{65,1},{129,193},{193,129... | collective-permute-start | bytes 196616 | tf_op jit(solution)/shard_map/ppermute | solution.py:29
  21.1 6.1 %collective-permute-start.3 = (bf16[128,512]{1,0:T(8,128)(2,1)S(1)}, bf16[128,512]{1,0:T(8,128)(2,1)S(1)}, u32[]{:S(2)}, u32[]{:S(2)}) collective-permute-start(bf16[128,512]{1,0:T(8,128)(2,1)S(1)} %get-tuple-element.8), channel_id=1, source_target_pairs={{0,64},{64,0},{128,192},{192,128},{1,65},{65,1},{129,193},{193,129... | collective-permute-start | bytes 393224 | tf_op jit(solution)/shard_map/ppermute | solution.py:29
  22.1 3.7 %collective-permute-start.7 = (bf16[128,256]{1,0:T(8,128)(2,1)S(1)}, bf16[128,256]{1,0:T(8,128)(2,1)S(1)}, u32[]{:S(2)}, u32[]{:S(2)}) collective-permute-start(bf16[128,256]{1,0:T(8,128)(2,1)S(1)} %shard_map.44), channel_id=1, source_target_pairs={{0,128},{64,192},{128,0},{192,64},{1,129},{65,193},{129,1},{193,65... | collective-permute-start | bytes 196616 | tf_op jit(solution)/shard_map/ppermute | solution.py:29
  22.8 4.4 %collective-permute-start.5 = (bf16[128,256]{1,0:T(8,128)(2,1)S(1)}, bf16[128,256]{1,0:T(8,128)(2,1)S(1)}, u32[]{:S(2)}, u32[]{:S(2)}) collective-permute-start(bf16[128,256]{1,0:T(8,128)(2,1)S(1)} %shard_map.42), channel_id=1, source_target_pairs={{0,128},{64,192},{128,0},{192,64},{1,129},{65,193},{129,1},{193,65... | collective-permute-start | bytes 196616 | tf_op jit(solution)/shard_map/ppermute | solution.py:29
